TPU v7x, 256 devices: a whole 4x4x8 slice. The times are simulated.
256 devices in a mesh: batch: 16 (over x, y_hi, core), space: 16 (over z, y_lo).
Axes of the slice: x: 4, y: 4 (y_hi: 2, y_lo: 2; y = y_hi * 2 + y_lo), z: 8, core: 2. Of those that a mesh axis runs over, the one named last changes fastest.
Arguments:
- snapshots: bfloat16 [16, 64, 32, 1024], P('batch', None, 'space'), may hold values from -6 to 6
- cotangent: bfloat16 [16, 64, 32, 1024], P('batch', None, 'space'), may hold values from -6 to 6
- mode_weight: bfloat16 [16, 16, 24, 64, 64], P('batch', 'space'), may hold values from -0.75 to 0.75
- conv_weight: bfloat16 [3, 3, 3, 64, 64], replicated, may hold values from -0.15625 to 0.15625
Outputs:
- activated: bfloat16 [16, 64, 32, 1024], P('batch', None, 'space')
- input_gradient: bfloat16 [16, 64, 32, 1024], P('batch', None, 'space')
- mode_gradient: float32 [16, 16, 24, 64, 64], P('batch', 'space')
- conv_gradient: float32 [3, 3, 3, 64, 64], replicated
All inputs are finite; a program needn't handle non-finite values.
Results may differ from a plain program's by a relative error of at most 0.02.
Values may be sent and summed in bfloat16 or wider, within the bound.
A program may use at most 128 MiB of HBM per device.

v0:
```python
import math

import jax
import jax.numpy as jnp
from jax import lax
from jax.sharding import PartitionSpec as P

KX = 8
KY = 8
KZ = 12
NX = 32
NY = 32


inv_root_two = 1.0 / math.sqrt(2.0)
inv_root_two_pi = 1.0 / math.sqrt(2.0 * math.pi)


def extended_2(cells, sides, width):
    for axis, dim in sides:
        count = lax.axis_size(axis)
        ends = count - 1
        head = lax.slice_in_dim(cells, 0, width, axis=dim)
        tail = lax.slice_in_dim(cells, cells.shape[dim] - width, cells.shape[dim], axis=dim)
        cells = jnp.concatenate(
            [
                lax.ppermute(tail, axis, [(i, (i + 1) % count) for i in range(ends)]),
                cells,
                lax.ppermute(head, axis, [((i + 1) % count, i) for i in range(ends)]),
            ],
            axis=dim,
        )
    return cells


def basis_rows(half_count, length):
    row_index = lax.broadcasted_iota(jnp.int32, (2 * half_count, length), 0)
    cell_index = lax.broadcasted_iota(jnp.int32, (2 * half_count, length), 1)
    frequency = jnp.where(row_index < half_count, row_index, row_index - half_count + 1)
    phases = (frequency * cell_index % length).astype(jnp.float32) * (2.0 * math.pi / length)
    return jnp.where(row_index < half_count, jnp.cos(phases), jnp.sin(phases))


def make_tables(count_x, count_y, count_z, length_x, length_y, length_z):
    across = basis_rows(count_x, length_x)
    along_y = basis_rows(count_y, length_y)
    depth_rows = basis_rows(count_z, length_z)
    modes_x = 2 * count_x
    modes_y = 2 * count_y
    outer_table = (across[:, None, :, None] * along_y[None, :, None, :]).reshape(
        modes_x * modes_y, length_x * length_y
    )
    plane_analysis = (outer_table * (2.0 / math.sqrt(length_x * length_y))).astype(jnp.bfloat16)
    plane_synthesis = (outer_table.T * (2.0 / math.sqrt(modes_x * modes_y))).astype(jnp.bfloat16)
    depth_analysis = (depth_rows * math.sqrt(2.0 / length_z)).astype(jnp.bfloat16)
    depth_synthesis = (depth_rows.T * math.sqrt(2.0 / (2 * count_z))).astype(jnp.bfloat16)
    return (plane_analysis, plane_synthesis, depth_analysis, depth_synthesis)


def rim(values):
    return extended_2(values, (("space", 1),), 1)


def widen(values):
    channels, depth_cells, plane = values.shape
    extended = rim(values)
    return jnp.pad(
        extended.reshape(channels, depth_cells + 2, NX, NY), ((0, 0), (0, 0), (1, 1), (1, 1))
    )


def to_pencils(values):
    return lax.all_to_all(values, "space", split_axis=3, concat_axis=1, tiled=True)


def to_slabs(values):
    return lax.all_to_all(values, "space", split_axis=1, concat_axis=3, tiled=True)


def stacked_window(padded, offset_x, offset_y):
    channels = padded.shape[0]
    depth_cells = padded.shape[1] - 2
    window = padded[:, :, offset_x : offset_x + NX, offset_y : offset_y + NY]
    stacked = jnp.stack([window[:, offset_z : offset_z + depth_cells] for offset_z in range(3)], 0)
    return stacked.reshape(3, channels, depth_cells * NX * NY)


def stencil(padded, kernel):
    depth_cells = padded.shape[1] - 2
    summed = jnp.zeros((kernel.shape[4], depth_cells * NX * NY), jnp.float32)
    for offset_x in range(3):
        for offset_y in range(3):
            stacked = stacked_window(padded, offset_x, offset_y)
            summed = summed + lax.dot_general(
                kernel[:, offset_x, offset_y],
                stacked,
                (((0, 1), (0, 1)), ((), ())),
                preferred_element_type=jnp.float32,
            )
    return summed


def kernel_terms(padded, pre_flat):
    pieces = []
    for offset_x in range(3):
        row_pieces = []
        for offset_y in range(3):
            stacked = stacked_window(padded, offset_x, offset_y)
            row_pieces.append(
                lax.dot_general(
                    stacked, pre_flat, (((2,), (1,)), ((), ())), preferred_element_type=jnp.float32
                )
            )
        pieces.append(jnp.stack(row_pieces, 1))
    return jnp.stack(pieces, 1)


def shards(snapshots, cotangent, mode_weight, conv_weight):
    local_field = snapshots[0]
    channels, depth_cells, plane = local_field.shape
    total_depth = depth_cells * lax.axis_size("space")
    modes_x = 2 * KX
    modes_y = 2 * KY
    plane_analysis, plane_synthesis, depth_analysis, depth_synthesis = make_tables(
        KX, KY, KZ, NX, NY, total_depth
    )
    padded = widen(local_field)
    plane_coef = lax.dot_general(
        local_field.reshape(channels * depth_cells, plane),
        plane_analysis,
        (((1,), (1,)), ((), ())),
        preferred_element_type=jnp.float32,
    )
    plane_coef = plane_coef.astype(jnp.bfloat16).reshape(channels, depth_cells, modes_x, modes_y)
    coef = jnp.einsum(
        "czxy,pz->cpxy", to_pencils(plane_coef), depth_analysis, preferred_element_type=jnp.float32
    ).astype(jnp.bfloat16)
    full_weight = lax.all_gather(mode_weight, "batch", axis=0, tiled=True)
    mixed = jnp.einsum(
        "ipxy,xypio->opxy", coef, full_weight, preferred_element_type=jnp.float32
    ).astype(jnp.bfloat16)
    depth_back = jnp.einsum(
        "opxy,zp->ozxy", mixed, depth_synthesis, preferred_element_type=jnp.float32
    ).astype(jnp.bfloat16)
    slab_back = to_slabs(depth_back)
    spectral = lax.dot_general(
        slab_back.reshape(channels * depth_cells, modes_x * modes_y),
        plane_synthesis,
        (((1,), (1,)), ((), ())),
        preferred_element_type=jnp.float32,
    )
    pre = spectral.reshape(channels, depth_cells * plane) + stencil(padded, conv_weight)
    normal_cdf = 0.5 * (1.0 + lax.erf(pre * inv_root_two))
    density = jnp.exp(-0.5 * pre * pre) * inv_root_two_pi
    activated = (pre * normal_cdf).astype(jnp.bfloat16).reshape(channels, depth_cells, plane)
    pre_grad = (
        cotangent[0].reshape(channels, depth_cells * plane).astype(jnp.float32)
        * (normal_cdf + pre * density)
    ).astype(jnp.bfloat16)
    back_plane = jnp.dot(
        pre_grad.reshape(channels * depth_cells, plane),
        plane_synthesis,
        preferred_element_type=jnp.float32,
    )
    back_plane = back_plane.astype(jnp.bfloat16).reshape(channels, depth_cells, modes_x, modes_y)
    mixed_grad = jnp.einsum(
        "ozxy,zp->opxy", to_pencils(back_plane), depth_synthesis, preferred_element_type=jnp.float32
    ).astype(jnp.bfloat16)
    coef_grad = jnp.einsum(
        "opxy,xypio->ipxy", mixed_grad, full_weight, preferred_element_type=jnp.float32
    ).astype(jnp.bfloat16)
    mode_gradient = lax.psum_scatter(
        jnp.einsum("ipxy,opxy->xypio", coef, mixed_grad, preferred_element_type=jnp.float32).astype(
            jnp.bfloat16
        ),
        "batch",
        scatter_dimension=0,
        tiled=True,
    ).astype(jnp.float32)
    depth_grad = jnp.einsum(
        "ipxy,pz->izxy", coef_grad, depth_analysis, preferred_element_type=jnp.float32
    ).astype(jnp.bfloat16)
    slab_grad = to_slabs(depth_grad)
    spectral_grad = jnp.dot(
        slab_grad.reshape(channels * depth_cells, modes_x * modes_y),
        plane_analysis,
        preferred_element_type=jnp.float32,
    )
    flipped = jnp.transpose(conv_weight[::-1, ::-1, ::-1], (0, 1, 2, 4, 3))
    local_grad = stencil(widen(pre_grad.reshape(channels, depth_cells, plane)), flipped)
    input_gradient = (
        (spectral_grad.reshape(channels, depth_cells * plane) + local_grad)
        .astype(jnp.bfloat16)
        .reshape(channels, depth_cells, plane)
    )
    kernel_local = kernel_terms(padded, pre_grad)
    kernel_total = lax.psum(kernel_local, ("batch", "space"))
    conv_gradient = kernel_total / math.sqrt(lax.axis_size("batch") * total_depth * plane)
    return (activated[None], input_gradient[None], mode_gradient, conv_gradient)


def solution(mesh):
    in_specs = (
        P("batch", None, "space", None),
        P("batch", None, "space", None),
        P("batch", "space", None, None, None),
        P(),
    )
    out_specs = (
        P("batch", None, "space", None),
        P("batch", None, "space", None),
        P("batch", "space", None, None, None),
        P(),
    )
    return jax.shard_map(shards, mesh=mesh, in_specs=in_specs, out_specs=out_specs, check_vma=False)
```

profile of v0, /device:TPU:1, one launch (start us, length us, event | category | flops | bytes accessed | tf_op | source)
XLA Modules:
  0.0 513.6 jit_solution(1458009510099474854)
XLA Ops:
  10.0 4.7 collective-permute-start
  17.9 2.2 fusion.6
  20.1 3.6 convert_element_type.165
  28.7 11.0 %all-to-all-start = ((bf16[16,2,1024]{2,1,0:T(2,128)(2,1)}), bf16[16,2,1024]{2,1,0:T(2,128)(2,1)S(1)}, u32[]{:S(2)}, u32[]{:S(2)}) async-start(bf16[16,2,1024]{2,1,0:T(2,128)(2,1)} %reshape.401), calls=%async_computation | async-start | bytes 131072 | tf_op jit(solution)/shard_map/all_to_all | solution.py:73
  42.4 2.9 convert_element_type.178
  45.3 2.3 all-to-all-done
  60.7 3.9 fusion.195
  64.6 2.0 copy.134
  66.6 2.0 copy.133
  80.1 2.0 copy.119
  82.1 2.0 copy.118
  98.3 4.6 fusion.3
  104.0 5.9 %all-to-all-start.1 = ((bf16[16,2,1024]{2,1,0:T(2,128)(2,1)}), bf16[16,2,1024]{2,1,0:T(2,128)(2,1)}, u32[]{:S(2)}, u32[]{:S(2)}) async-start(bf16[16,2,1024]{2,1,0:T(2,128)(2,1)} %reshape.403), calls=%async_computation.1 | async-start | bytes 131072 | tf_op jit(solution)/shard_map/all_to_all | solution.py:77
  110.0 2.4 fusion.13
  115.2 2.8 all-to-all-done.1
  120.7 2.6 fusion.85
  123.3 2.1 convolution_bitcast_fusion.25
  135.3 4.8 all-to-all-start.2
  141.5 6.6 %all-to-all-done.2 = bf16[16,2,1024]{2,1,0:T(2,128)(2,1)S(1)} async-done(((bf16[16,2,1024]{2,1,0:T(2,128)(2,1)}), bf16[16,2,1024]{2,1,0:T(2,128)(2,1)S(1)}, u32[]{:S(2)}, u32[]{:S(2)}) %all-to-all-start.2) | async-done | bytes 65568 | tf_op jit(solution)/shard_map/all_to_all | solution.py:73
  148.7 5.8 %fusion = bf16[16,1,24,64,64]{4,3,2,1,0:T(8,128)(2,1)} fusion(f32[16,24,64]{2,1,0:T(8,128)S(1)} %get-tuple-element.76, f32[16,24,64]{2,1,0:T(8,128)S(1)} %get-tuple-element.77), kind=kLoop, calls=%fused_computation.1 | loop fusion | flops 3145728 | bytes 3342336 | tf_op jit(solution)/shard_map/convert_element_type | solution.py:173
  157.6 2.3 collective-permute-start.2
  161.2 6.1 %fusion.1 = bf16[24,16,1,64]{3,2,1,0:T(2,128)(2,1)S(1)} fusion(bf16[64,24,16,1]{0,1,2,3:T(8,128)(2,1)S(1)} %bitcast.459, bf16[16,1,24,64,64]{4,3,2,1,0:T(8,128)(2,1)} %all-gather.2.cloned.1.call-done), kind=kOutput, calls=%fused_computation.4 | convolution fusion | flops 3145728 | bytes 3244032 | tf_op jit(solution)/shard_map/opxy,xypio->ipxy/dot_general | solution.py:169
  168.5 6.2 %all-to-all-start.3 = ((bf16[16,2,1024]{2,1,0:T(2,128)(2,1)}), bf16[16,2,1024]{2,1,0:T(2,128)(2,1)S(1)}, u32[]{:S(2)}, u32[]{:S(2)}) async-start(bf16[16,2,1024]{2,1,0:T(2,128)(2,1)} %reshape.407), calls=%async_computation.3 | async-start | bytes 131072 | tf_op jit(solution)/shard_map/all_to_all | solution.py:77
  186.4 3.8 fusion.193
  191.6 2.0 copy.172
  205.1 2.0 copy.164
  211.0 2.0 copy.159
  222.1 2.3 convolution_bitcast_fusion.1
  230.0 175.3 %all-reduce.4.cloned.1.call-done = f32[3,3,3,64,64]{4,3,0,2,1:T(8,128)} async-done(((f32[3,3,3,64,64]{4,3,0,2,1:T(8,128)}), f32[3,3,3,64,64]{4,3,0,2,1:T(8,128)}) %all-reduce.4.cloned.1.call-update) | async-done | bytes 442384 | tf_op jit(solution)/shard_map/psum | solution.py:197
  409.4 2.4 fusion.30
  412.7 92.2 %reduce-scatter.2.cloned.1.call-done = bf16[1,1,24,64,64]{4,3,2,1,0:T(8,128)(2,1)} async-done(((bf16[16,1,24,64,64]{4,3,2,1,0:T(8,128)(2,1)}), bf16[1,1,24,64,64]{4,3,2,1,0:T(8,128)(2,1)}) %reduce-scatter.2.cloned.1.call-update) | async-done | bytes 196624 | tf_op jit(solution)/shard_map/reduce_scatter | solution.py:172
  504.9 2.0 convert_element_type.196
  (325 shorter events, 123.8 us)
Async XLA Ops:
  7.2 91.1 %all-gather.2.cloned.1.call-start = ((), (), s32[]{:S(2)}) async-start(), calls=%async_computation.5 | async-start | bytes 6684672 | tf_op jit(solution)/shard_map/all_gather | solution.py:138
  10.0 38.8 %collective-permute-start = (bf16[64,1,1024]{0,2,1:T(8,128)(2,1)}, bf16[64,1,1024]{0,2,1:T(8,128)(2,1)}, u32[]{:S(2)}, u32[]{:S(2)}) collective-permute-start(bf16[64,1,1024]{0,2,1:T(8,128)(2,1)} %get-tuple-element.72), channel_id=1, source_target_pairs={{0,1},{1,2},{2,3},{3,4},{4,5},{5,6},{6,7},{7,8},{8,9},{9,10},{10,1... | collective-permute-start | bytes 393224 | tf_op jit(solution)/shard_map/ppermute | solution.py:27
  14.7 34.1 %collective-permute-start.1 = (bf16[64,1,1024]{0,2,1:T(8,128)(2,1)}, bf16[64,1,1024]{0,2,1:T(8,128)(2,1)}, u32[]{:S(2)}, u32[]{:S(2)}) collective-permute-start(bf16[64,1,1024]{0,2,1:T(8,128)(2,1)} %get-tuple-element.73), channel_id=1, source_target_pairs={{1,0},{2,1},{3,2},{4,3},{5,4},{6,5},{7,6},{8,7},{9,8},{10,9},{11,1... | collective-permute-start | bytes 393224 | tf_op jit(solution)/shard_map/ppermute | solution.py:29
  20.1 19.6 %copy-start.1 = (bf16[1,64,2,1024]{3,2,1,0:T(2,128)(2,1)S(1)}, bf16[1,64,2,1024]{3,2,1,0:T(2,128)(2,1)}, u32[]{:S(2)}) copy-start(bf16[1,64,2,1024]{3,2,1,0:T(2,128)(2,1)} %param.4) | copy-start | bytes 786436
  28.7 18.9 %all-to-all-start = ((bf16[16,2,1024]{2,1,0:T(2,128)(2,1)}), bf16[16,2,1024]{2,1,0:T(2,128)(2,1)S(1)}, u32[]{:S(2)}, u32[]{:S(2)}) async-start(bf16[16,2,1024]{2,1,0:T(2,128)(2,1)} %reshape.401), calls=%async_computation | async-start | bytes 131072 | tf_op jit(solution)/shard_map/all_to_all | solution.py:73
  64.6 13.7 %copy-start.9 = (bf16[64,2,32,32]{0,3,2,1:T(8,128)(2,1)S(1)}, bf16[64,2,32,32]{0,3,2,1:T(8,128)(2,1)}, u32[]{:S(2)}) copy-start(bf16[64,2,32,32]{0,3,2,1:T(8,128)(2,1)} %get-tuple-element.49) | copy-start | bytes 786436
  66.6 12.6 %copy-start.7 = (bf16[64,2,32,32]{0,3,2,1:T(8,128)(2,1)S(1)}, bf16[64,2,32,32]{0,3,2,1:T(8,128)(2,1)}, u32[]{:S(2)}) copy-start(bf16[64,2,32,32]{0,3,2,1:T(8,128)(2,1)} %get-tuple-element.50) | copy-start | bytes 786436
  79.2 11.6 %copy-start.5 = (bf16[64,2,32,32]{0,3,2,1:T(8,128)(2,1)S(1)}, bf16[64,2,32,32]{0,3,2,1:T(8,128)(2,1)}, u32[]{:S(2)}) copy-start(bf16[64,2,32,32]{0,3,2,1:T(8,128)(2,1)} %get-tuple-element.57) | copy-start | bytes 786436
  80.1 11.6 %copy-start.3 = (bf16[64,2,32,32]{0,3,2,1:T(8,128)(2,1)S(1)}, bf16[64,2,32,32]{0,3,2,1:T(8,128)(2,1)}, u32[]{:S(2)}) copy-start(bf16[64,2,32,32]{0,3,2,1:T(8,128)(2,1)} %get-tuple-element.58) | copy-start | bytes 786436
  82.1 10.5 %copy-start.22 = (bf16[1,64,2048]{2,1,0:T(8,128)(2,1)S(1)}, bf16[1,64,2048]{2,1,0:T(8,128)(2,1)}, u32[]{:S(2)}) copy-start(bf16[1,64,2048]{2,1,0:T(8,128)(2,1)} %copy.107) | copy-start | bytes 786436
  98.3 11.7 %copy-start.30 = (bf16[1,64,2048]{2,1,0:T(8,128)(2,1)S(1)}, bf16[1,64,2048]{2,1,0:T(8,128)(2,1)}, u32[]{:S(2)}) copy-start(bf16[1,64,2048]{2,1,0:T(8,128)(2,1)} %copy.134) | copy-start | bytes 786436
  98.3 11.7 %copy-start.32 = (bf16[1,64,2048]{2,1,0:T(8,128)(2,1)S(1)}, bf16[1,64,2048]{2,1,0:T(8,128)(2,1)}, u32[]{:S(2)}) copy-start(bf16[1,64,2048]{2,1,0:T(8,128)(2,1)} %copy.133) | copy-start | bytes 786436
  102.8 10.4 %copy-start.2 = (bf16[64,2,32,32]{0,3,2,1:T(8,128)(2,1)S(1)}, bf16[64,2,32,32]{0,3,2,1:T(8,128)(2,1)}, u32[]{:S(2)}) copy-start(bf16[64,2,32,32]{0,3,2,1:T(8,128)(2,1)} %get-tuple-element.40) | copy-start | bytes 786436
  104.0 13.9 %all-to-all-start.1 = ((bf16[16,2,1024]{2,1,0:T(2,128)(2,1)}), bf16[16,2,1024]{2,1,0:T(2,128)(2,1)}, u32[]{:S(2)}, u32[]{:S(2)}) async-start(bf16[16,2,1024]{2,1,0:T(2,128)(2,1)} %reshape.403), calls=%async_computation.1 | async-start | bytes 131072 | tf_op jit(solution)/shard_map/all_to_all | solution.py:77
  110.0 10.2 %copy-start = (bf16[256,1024]{1,0:T(8,128)(2,1)S(1)}, bf16[256,1024]{1,0:T(8,128)(2,1)}, u32[]{:S(2)}) copy-start(bf16[256,1024]{1,0:T(8,128)(2,1)} %convert_element_type.178) | copy-start | bytes 1572868
  123.3 33.1 %copy-start.13 = (bf16[64,2048]{1,0:T(8,128)(2,1)}, bf16[64,2048]{1,0:T(8,128)(2,1)S(1)}, u32[]{:S(2)}) copy-start(bf16[64,2048]{1,0:T(8,128)(2,1)S(1)} %get-tuple-element.68) | copy-start | bytes 786436
  132.7 7.6 %copy-start.89 = (f32[3,1,64,64]{3,2,0,1:T(8,128)S(1)}, f32[3,1,64,64]{3,2,0,1:T(8,128)}, u32[]{:S(2)}) copy-start(f32[3,1,64,64]{3,2,0,1:T(8,128)} %convolution_bitcast_fusion.19) | copy-start | bytes 147460
  132.7 7.6 %copy-start.83 = (f32[3,1,64,64]{3,2,0,1:T(8,128)S(1)}, f32[3,1,64,64]{3,2,0,1:T(8,128)}, u32[]{:S(2)}) copy-start(f32[3,1,64,64]{3,2,0,1:T(8,128)} %convolution_bitcast_fusion.25) | copy-start | bytes 147460
  132.7 7.6 %copy-start.84 = (f32[3,1,64,64]{3,2,0,1:T(8,128)S(1)}, f32[3,1,64,64]{3,2,0,1:T(8,128)}, u32[]{:S(2)}) copy-start(f32[3,1,64,64]{3,2,0,1:T(8,128)} %convolution_bitcast_fusion.24) | copy-start | bytes 147460
  132.7 7.6 %copy-start.85 = (f32[3,1,64,64]{3,2,0,1:T(8,128)S(1)}, f32[3,1,64,64]{3,2,0,1:T(8,128)}, u32[]{:S(2)}) copy-start(f32[3,1,64,64]{3,2,0,1:T(8,128)} %convolution_bitcast_fusion.23) | copy-start | bytes 147460
  132.7 7.6 %copy-start.86 = (f32[3,1,64,64]{3,2,0,1:T(8,128)S(1)}, f32[3,1,64,64]{3,2,0,1:T(8,128)}, u32[]{:S(2)}) copy-start(f32[3,1,64,64]{3,2,0,1:T(8,128)} %convolution_bitcast_fusion.22) | copy-start | bytes 147460
  132.7 7.6 %copy-start.87 = (f32[3,1,64,64]{3,2,0,1:T(8,128)S(1)}, f32[3,1,64,64]{3,2,0,1:T(8,128)}, u32[]{:S(2)}) copy-start(f32[3,1,64,64]{3,2,0,1:T(8,128)} %convolution_bitcast_fusion.21) | copy-start | bytes 147460
  135.3 12.7 %all-to-all-start.2 = ((bf16[16,2,1024]{2,1,0:T(2,128)(2,1)}), bf16[16,2,1024]{2,1,0:T(2,128)(2,1)S(1)}, u32[]{:S(2)}, u32[]{:S(2)}) async-start(bf16[16,2,1024]{2,1,0:T(2,128)(2,1)} %reshape.405), calls=%async_computation.2 | async-start | bytes 131072 | tf_op jit(solution)/shard_map/all_to_all | solution.py:73
  140.2 265.1 %all-reduce.4.cloned.1.call-start = ((), (), s32[]{:S(2)}) async-start(), calls=%async_computation.7 | async-start | bytes 1769472 | tf_op jit(solution)/shard_map/psum | solution.py:197
  141.4 363.5 %reduce-scatter.2.cloned.1.call-start = ((), (), s32[]{:S(2)}) async-start(), calls=%async_computation.6 | async-start | bytes 6684672 | tf_op jit(solution)/shard_map/reduce_scatter | solution.py:172
  157.6 17.1 %collective-permute-start.2 = (bf16[64,1,1024]{0,2,1:T(8,128)(2,1)S(1)}, bf16[64,1,1024]{0,2,1:T(8,128)(2,1)S(1)}, u32[]{:S(2)}, u32[]{:S(2)}) collective-permute-start(bf16[64,1,1024]{0,2,1:T(8,128)(2,1)S(1)} %get-tuple-element.66), channel_id=1, source_target_pairs={{0,1},{1,2},{2,3},{3,4},{4,5},{5,6},{6,7},{7,8},{8,9},{9,10},{10,1... | collective-permute-start | bytes 393224 | tf_op jit(solution)/shard_map/ppermute | solution.py:27
  159.9 14.8 %collective-permute-start.3 = (bf16[64,1,1024]{0,2,1:T(8,128)(2,1)S(1)}, bf16[64,1,1024]{0,2,1:T(8,128)(2,1)S(1)}, u32[]{:S(2)}, u32[]{:S(2)}) collective-permute-start(bf16[64,1,1024]{0,2,1:T(8,128)(2,1)S(1)} %get-tuple-element.67), channel_id=1, source_target_pairs={{1,0},{2,1},{3,2},{4,3},{5,4},{6,5},{7,6},{8,7},{9,8},{10,9},{11,1... | collective-permute-start | bytes 393224 | tf_op jit(solution)/shard_map/ppermute | solution.py:29
  168.5 239.1 %all-to-all-start.3 = ((bf16[16,2,1024]{2,1,0:T(2,128)(2,1)}), bf16[16,2,1024]{2,1,0:T(2,128)(2,1)S(1)}, u32[]{:S(2)}, u32[]{:S(2)}) async-start(bf16[16,2,1024]{2,1,0:T(2,128)(2,1)} %reshape.407), calls=%async_computation.3 | async-start | bytes 131072 | tf_op jit(solution)/shard_map/all_to_all | solution.py:77
  190.3 13.0 %copy-start.10 = (bf16[64,2,32,32]{0,3,2,1:T(8,128)(2,1)S(1)}, bf16[64,2,32,32]{0,3,2,1:T(8,128)(2,1)}, u32[]{:S(2)}) copy-start(bf16[64,2,32,32]{0,3,2,1:T(8,128)(2,1)} %get-tuple-element.23) | copy-start | bytes 786436
  191.6 12.6 %copy-start.8 = (bf16[64,2,32,32]{0,3,2,1:T(8,128)(2,1)S(1)}, bf16[64,2,32,32]{0,3,2,1:T(8,128)(2,1)}, u32[]{:S(2)}) copy-start(bf16[64,2,32,32]{0,3,2,1:T(8,128)(2,1)} %get-tuple-element.24) | copy-start | bytes 786436
  204.2 11.6 %copy-start.6 = (bf16[64,2,32,32]{0,3,2,1:T(8,128)(2,1)S(1)}, bf16[64,2,32,32]{0,3,2,1:T(8,128)(2,1)}, u32[]{:S(2)}) copy-start(bf16[64,2,32,32]{0,3,2,1:T(8,128)(2,1)} %get-tuple-element.31) | copy-start | bytes 786436
  205.1 11.6 %copy-start.4 = (bf16[64,2,32,32]{0,3,2,1:T(8,128)(2,1)S(1)}, bf16[64,2,32,32]{0,3,2,1:T(8,128)(2,1)}, u32[]{:S(2)}) copy-start(bf16[64,2,32,32]{0,3,2,1:T(8,128)(2,1)} %get-tuple-element.32) | copy-start | bytes 786436
  (70 other events, 212.8 us)
Sparse Core Ops, SparseCore 0:
  10.7 73.2 all-gather.1
  147.1 258.1 all-reduce.3
  410.4 94.5 reduce-scatter.1
where the time goes:
time: 520 us; the launch traced here: 514 us
  waiting for transfers between devices  280 us (54%)
  local copies, waits for them, and re-layouts  117 us (22%)
  matrix products  47.2 us (9%)
  starting transfers between devices  37.6 us (7%)
  other arithmetic  17.1 us (3%)
  between operations  15.2 us (3%)
    psum x1, waiting for transfers between devices, shards(): kernel_total = lax.psum(kernel_local, ('batch', 'space'))  175 us
    reduce_scatter x1, waiting for transfers between devices, shards(): lax.psum_scatter(jnp.einsum('ipxy,opxy->xypio', coef, mixed_grad, preferr...  92.2 us
    another operation x53, local copies, waits for them, and re-layouts, stacked_window(): jnp.stack([window[:, offset_z:offset_z + depth_cells] for offset_z in ran...  76.6 us
    dot_general x18, matrix products, stencil(): lax.dot_general(kernel[:, offset_x, offset_y], stacked, (((0, 1), (0, 1))...  22.9 us
    all_to_all x2, starting transfers between devices, to_pencils(): lax.all_to_all(values, 'space', split_axis=3, concat_axis=1, tiled=True)  15.8 us
    all_to_all x2, starting transfers between devices, to_slabs(): lax.all_to_all(values, 'space', split_axis=1, concat_axis=3, tiled=True)  12.1 us
    slice x4, local copies, waits for them, and re-layouts, stacked_window(): window[:, offset_z:offset_z + depth_cells]  10.7 us
  transfers between devices with their start and end apart: 11, of which 5 were waited for; matrix products, arithmetic and copies ran while one was open for 30% of the time, Pallas kernels for 0%

commit v1 on v0

v1 whole, which is shorter than its diff:
```python
import math

import jax
import jax.numpy as jnp
import ml_dtypes
import numpy as np
from jax import lax
from jax.experimental import pallas as pl
from jax.experimental.pallas import tpu as pltpu
from jax.sharding import PartitionSpec as P

KX = 8
KY = 8
KZ = 12
NX = 32
NY = 32
NZ = 32
PLANE = NX * NY
C = 64
G = 16
SNAPS = 16

MESH = pl.DeviceIdType.MESH
F32 = jnp.float32
BF16 = jnp.bfloat16

inv_root_two = 1.0 / math.sqrt(2.0)
inv_root_two_pi = 1.0 / math.sqrt(2.0 * math.pi)
conv_scale = 1.0 / math.sqrt(SNAPS * NZ * PLANE)


def basis_rows(half_count, length):
    rows = np.arange(2 * half_count)[:, None]
    cells = np.arange(length)[None, :]
    frequency = np.where(rows < half_count, rows, rows - half_count + 1)
    phases = ((frequency * cells) % length).astype(np.float32) * np.float32(2.0 * math.pi / length)
    return np.where(rows < half_count, np.cos(phases), np.sin(phases)).astype(np.float32)


def make_tables():
    across = basis_rows(KX, NX)
    along_y = basis_rows(KY, NY)
    depth_rows = basis_rows(KZ, NZ)
    outer = across[None, :, :, None] * along_y[:, None, None, :]
    plane = (outer.reshape(256, PLANE) * np.float32(2.0 / math.sqrt(PLANE))).astype(ml_dtypes.bfloat16)
    analysis = (depth_rows * np.float32(math.sqrt(2.0 / NZ))).astype(ml_dtypes.bfloat16)
    synthesis = (depth_rows.T * np.float32(math.sqrt(2.0 / (2 * KZ)))).astype(ml_dtypes.bfloat16)
    to_modes = np.zeros((2, G, 16, 2, G, 16), ml_dtypes.bfloat16)
    to_cells = np.zeros((2, G, 16, 2, G, 16), ml_dtypes.bfloat16)
    down = analysis.reshape(2, KZ, 16, 2).transpose(0, 1, 3, 2)
    up = synthesis.reshape(16, 2, 2, KZ).transpose(1, 0, 2, 3)
    for mode in range(16):
        to_modes[:, mode, :KZ, :, :, mode] = down
        to_cells[:, :, mode, :, mode, :KZ] = up
    to_modes = to_modes.reshape(512, 512)
    to_cells = to_cells.reshape(512, 512)
    depth = np.stack([to_modes, to_cells, to_cells.T, to_modes.T])
    swap = np.zeros((16, 16, 16, 16), ml_dtypes.bfloat16)
    for a in range(16):
        for b in range(16):
            swap[a, b, b, a] = 1
    x = np.arange(PLANE) // NY
    y = np.arange(PLANE) % NY
    inside = np.zeros((16, PLANE), ml_dtypes.bfloat16)
    for tap in range(9):
        dx, dy = tap // 3 - 1, tap % 3 - 1
        inside[tap] = (x + dx >= 0) & (x + dx < NX) & (y + dy >= 0) & (y + dy < NY)
    return plane, depth, swap.reshape(256, 256), inside


def mm(left, right, left_dim=1, right_dim=0):
    return lax.dot_general(
        left, right, (((left_dim,), (right_dim,)), ((), ())), preferred_element_type=F32
    )


def kernel(
    x_in, cot_in, w_in, cw_in, plane_in, depth_in, swap_in, inside_in,
    act_out, grad_out, mode_out, conv_out,
    x, cot, w, cw, plane, depth, swap, inside,
    act, grad, mode, conv,
    send, recv, halo, pre_halo, cols, forward_w, back_w, mix_w, total, pg, coef, coef_back,
    part_send, part_recv, term_send, term_recv, full_send, full_recv,
    in_sem, out_sem, send_sem, recv_sem, halo_sem, sum_send_sem, sum_recv_sem,
):
    me_b = lax.axis_index("batch")
    me_s = lax.axis_index("space")
    mine = {"batch": me_b, "space": me_s}

    loads = [
        pltpu.make_async_copy(source, target, in_sem.at[i])
        for i, (source, target) in enumerate(
            (
                (x_in, x), (plane_in, plane), (depth_in, depth), (inside_in, inside),
                (cw_in, cw), (swap_in, swap), (w_in, w), (cot_in, cot),
            )
        )
    ]
    for load in loads:
        load.start()

    barrier = pltpu.get_barrier_semaphore()

    def greet(step, carry):
        for axis in ("space", "batch"):
            peer = lax.rem(mine[axis] + step, G)
            pl.semaphore_signal(barrier, inc=1, device_id={axis: peer}, device_id_type=MESH)
        return carry

    lax.fori_loop(1, G, greet, 0)

    def tile_copy(phase, axis, source, slot):
        return pltpu.make_async_remote_copy(
            src_ref=send.at[phase, source],
            dst_ref=recv.at[phase, slot],
            send_sem=send_sem.at[phase, source],
            recv_sem=recv_sem.at[phase, slot],
            device_id={axis: source},
            device_id_type=MESH,
        )

    def exchange_start(phase, axis, value):
        me = mine[axis]
        send[phase] = value.reshape(G, 16, 128)
        recv[phase, me] = send[phase, me]

        def step(i, carry):
            tile_copy(phase, axis, lax.rem(me + i, G), me).start()
            return carry

        lax.fori_loop(1, G, step, 0)

    def exchange_wait(phase, axis):
        me = mine[axis]

        def step(i, carry):
            peer = lax.rem(me + i, G)
            tile_copy(phase, axis, peer, peer).wait_recv()
            return carry

        lax.fori_loop(1, G, step, 0)
        return recv[phase].reshape(256, 128)

    def exchange_drain(phase, axis):
        me = mine[axis]

        def step(i, carry):
            tile_copy(phase, axis, lax.rem(me + i, G), me).wait_send()
            return carry

        lax.fori_loop(1, G, step, 0)

    def halo_copy(source, target, slot, which, offset):
        return pltpu.make_async_remote_copy(
            src_ref=source,
            dst_ref=target.at[slot],
            send_sem=halo_sem.at[0, which],
            recv_sem=halo_sem.at[1, which],
            device_id={"space": lax.rem(me_s + offset, G)},
            device_id_type=MESH,
        )

    def depth_transform(which, tiles):
        stacked = jnp.concatenate([tiles[:, :C], tiles[:, C:]], axis=0)
        both = mm(depth[which], stacked)
        return jnp.concatenate([both[:256], both[256:]], axis=1).astype(BF16)

    def spread(layer, cells):
        for tap in range(9):
            shift = (tap // 3 - 1) * NY + (tap % 3 - 1)
            moved = cells
            if shift:
                moved = pltpu.roll(cells, (-shift) % PLANE, 1) * inside[tap : tap + 1, :]
            cols[tap * C : (tap + 1) * C, layer * PLANE : (layer + 1) * PLANE] = moved

    def stencil(weights):
        width = 256
        for chunk in range(PLANE // width):
            lanes = [pl.ds(layer * PLANE + chunk * width, width) for layer in range(4)]
            acc = mm(weights[C : 3 * C, :], cols[:, lanes[1]])
            acc = acc + mm(weights[0 : 2 * C, :], cols[:, lanes[2]])
            first = mm(weights[2 * C : 3 * C, :], cols[:, lanes[0]])
            last = mm(weights[0:C, :], cols[:, lanes[3]])
            total[:, pl.ds(chunk * width, width)] = acc + jnp.concatenate([first, last], axis=0)

    loads[0].wait()
    loads[1].wait()
    both_layers = jnp.concatenate([x[:, :PLANE], x[:, PLANE:]], axis=0)
    plane_coef = mm(plane[...], both_layers, 1, 1).astype(BF16)
    pl.semaphore_wait(barrier, 2 * (G - 1))
    exchange_start(0, "space", plane_coef)
    halos = [
        halo_copy(x.at[:, pl.ds(PLANE, PLANE)], halo, 0, 0, 1),
        halo_copy(x.at[:, pl.ds(0, PLANE)], halo, 1, 1, G - 1),
    ]
    for copy in halos:
        copy.start()

    loads[2].wait()
    loads[3].wait()
    spread(1, x[:, :PLANE])
    tiles = exchange_wait(0, "space")
    exchange_start(1, "batch", depth_transform(0, tiles))

    loads[4].wait()
    for a in range(3):
        for tap in range(9):
            block = cw[a, tap]
            forward_w[(2 - a) * C : (3 - a) * C, tap * C : (tap + 1) * C] = (
                block.astype(F32).T.astype(BF16)
            )
            back_w[a * C : (a + 1) * C, (8 - tap) * C : (9 - tap) * C] = block
    loads[5].wait()
    loads[6].wait()
    mix_w[...] = jnp.zeros_like(mix_w)
    for p in range(KZ):
        mix_w[p, :C, :C] = w[p]
        mix_w[p, C:, C:] = w[KZ + p]

    tiles = exchange_wait(1, "batch")
    coef[...] = mm(swap[...], tiles).astype(BF16)

    def rows_of(p):
        return pl.ds(p * 16, 16)

    def pad_and_swap(pieces):
        value = jnp.concatenate(pieces + [jnp.zeros((64, 128), F32)], axis=0).astype(BF16)
        return mm(swap[...], value).astype(BF16)

    mixed = [mm(coef[rows_of(p), :], mix_w[p]) for p in range(KZ)]
    exchange_start(2, "batch", pad_and_swap(mixed))

    spread(2, x[:, PLANE:])
    for copy in halos:
        copy.wait_recv()
    spread(0, jnp.where(me_s > 0, halo[0], jnp.zeros_like(halo[0])))
    spread(3, jnp.where(me_s < G - 1, halo[1], jnp.zeros_like(halo[1])))

    tiles = exchange_wait(2, "batch")
    exchange_start(3, "space", depth_transform(1, tiles))
    stencil(forward_w)
    loads[7].wait()
    tiles = exchange_wait(3, "space")
    doubled = tiles * jnp.asarray(2.0, BF16)

    for chunk in range(4):
        lanes = pl.ds(chunk * 256, 256)
        total[:, lanes] += mm(doubled, plane[:, lanes], 0, 0)
    for layer in range(2):
        for chunk in range(4):
            lanes = pl.ds(chunk * 256, 256)
            cells = pl.ds(layer * PLANE + chunk * 256, 256)
            rows = pl.ds(layer * C, C)
            pre = total[rows, lanes]
            normal_cdf = 0.5 * (1.0 + lax.erf(pre * inv_root_two))
            density = jnp.exp(-0.5 * pre * pre) * inv_root_two_pi
            act[:, cells] = (pre * normal_cdf).astype(BF16)
            pg[rows, lanes] = (
                cot[:, cells].astype(F32) * (normal_cdf + pre * density)
            ).astype(BF16)
    stores = [pltpu.make_async_copy(act, act_out, out_sem.at[0])]
    stores[0].start()

    back_plane = (mm(plane[...], pg[...], 1, 1) * 2.0).astype(BF16)
    exchange_start(4, "space", back_plane)
    pre_halos = [
        halo_copy(pg.at[pl.ds(C, C), :], pre_halo, 0, 2, 1),
        halo_copy(pg.at[pl.ds(0, C), :], pre_halo, 1, 3, G - 1),
    ]
    for copy in pre_halos:
        copy.start()

    for r in range(3):
        rows = pl.ds(r * 192, 192)
        by_layer = [
            mm(cols[rows, pl.ds(layer * PLANE, PLANE)], pg[...], 1, 1) for layer in range(4)
        ]
        terms = [by_layer[a][:, :C] + by_layer[a + 1][:, C:] for a in range(3)]
        part_send[rows, :] = jnp.concatenate(terms[:2], axis=1).astype(BF16)
        part_send[pl.ds(576 + r * 96, 96), :] = jnp.concatenate(
            [terms[2][:96], terms[2][96:]], axis=1
        ).astype(BF16)
    part_send[pl.ds(864, 160), :] = jnp.zeros((160, 128), BF16)

    def sum_copy(stage, axis, source, target, peer, slot):
        return pltpu.make_async_remote_copy(
            src_ref=source,
            dst_ref=target.at[slot],
            send_sem=sum_send_sem.at[stage, peer],
            recv_sem=sum_recv_sem.at[stage, slot],
            device_id={axis: peer},
            device_id_type=MESH,
        )

    def part_rows(i):
        return part_send.at[pl.ds(pl.multiple_of(i * 64, 64), 64), :]

    stages = (
        ("space", part_rows, part_recv),
        ("batch", lambda i: term_send, term_recv),
        ("space", lambda i: full_send, full_recv),
    )

    def sum_start(stage):
        axis, source, target = stages[stage]
        me = mine[axis]
        target[me] = source(me)[...]

        def step(i, carry):
            peer = lax.rem(me + i, G)
            sum_copy(stage, axis, source(peer), target, peer, me).start()
            return carry

        lax.fori_loop(1, G, step, 0)

    def sum_wait(stage):
        axis, source, target = stages[stage]
        me = mine[axis]

        def step(i, carry):
            peer = lax.rem(me + i, G)
            sum_copy(stage, axis, source(peer), target, peer, peer).wait_recv()
            return carry

        lax.fori_loop(1, G, step, 0)

    def sum_drain(stage):
        axis, source, target = stages[stage]
        me = mine[axis]

        def step(i, carry):
            peer = lax.rem(me + i, G)
            sum_copy(stage, axis, source(peer), target, peer, me).wait_send()
            return carry

        lax.fori_loop(1, G, step, 0)

    def added(target):
        value = target[0].astype(F32)
        for i in range(1, G):
            value = value + target[i].astype(F32)
        return value

    tiles = exchange_wait(4, "space")
    exchange_start(5, "batch", depth_transform(2, tiles))
    sum_start(0)

    spread(1, pg[:C, :])
    tiles = exchange_wait(5, "batch")
    coef_back[...] = mm(swap[...], tiles).astype(BF16)
    gradients = [mm(coef_back[rows_of(p), :], mix_w[p], 1, 1) for p in range(KZ)]
    exchange_start(6, "batch", pad_and_swap(gradients))

    for p in range(KZ):
        product = mm(coef[rows_of(p), :], coef_back[rows_of(p), :], 0, 0)
        mode[p] = product[:C, :C]
        mode[KZ + p] = product[C:, C:]
    stores.append(pltpu.make_async_copy(mode, mode_out, out_sem.at[1]))
    stores[1].start()

    spread(2, pg[C:, :])
    sum_wait(0)
    term_send[...] = added(part_recv).astype(BF16)
    sum_start(1)

    tiles = exchange_wait(6, "batch")
    exchange_start(7, "space", depth_transform(3, tiles))

    for copy in pre_halos:
        copy.wait_recv()
    spread(0, jnp.where(me_s > 0, pre_halo[0], jnp.zeros_like(pre_halo[0])))
    spread(3, jnp.where(me_s < G - 1, pre_halo[1], jnp.zeros_like(pre_halo[1])))
    sum_wait(1)
    full_send[...] = (added(term_recv) * conv_scale).astype(BF16)
    sum_start(2)
    stencil(back_w)

    tiles = exchange_wait(7, "space")
    for chunk in range(4):
        lanes = pl.ds(chunk * 256, 256)
        value = (total[:, lanes] + mm(tiles, plane[:, lanes], 0, 0)).astype(BF16)
        grad[:, lanes] = value[:C]
        grad[:, pl.ds(PLANE + chunk * 256, 256)] = value[C:]
    stores.append(pltpu.make_async_copy(grad, grad_out, out_sem.at[2]))
    stores[2].start()

    sum_wait(2)
    for i in range(9):
        value = full_recv[i].astype(F32)
        conv[pl.ds(i * 64, 64), :] = value[:, :C]
        conv[pl.ds(576 + i * 64, 64), :] = value[:, C:]
    rest = full_recv[9:14].reshape(320, 128).astype(F32)
    for r in range(3):
        conv[pl.ds(1152 + r * 192, 96), :] = rest[r * 96 : (r + 1) * 96, :C]
        conv[pl.ds(1152 + r * 192 + 96, 96), :] = rest[r * 96 : (r + 1) * 96, C:]
    stores.append(pltpu.make_async_copy(conv, conv_out, out_sem.at[3]))
    stores[3].start()

    for phase, axis in enumerate(("space", "batch", "batch", "space") * 2):
        exchange_drain(phase, axis)
    for stage in range(3):
        sum_drain(stage)
    for copy in halos + pre_halos:
        copy.wait_send()
    for store in stores:
        store.wait()


def shards(snapshots, cotangent, mode_weight, conv_weight):
    plane, depth, swap, inside = make_tables()
    any_space = pl.BlockSpec(memory_space=pl.ANY)
    vmem = pltpu.VMEM
    dma = pltpu.SemaphoreType.DMA
    outs = pl.pallas_call(
        kernel,
        name="layer",
        out_shape=(
            jax.ShapeDtypeStruct((C, 2 * PLANE), BF16),
            jax.ShapeDtypeStruct((C, 2 * PLANE), BF16),
            jax.ShapeDtypeStruct((2 * KZ, C, C), F32),
            jax.ShapeDtypeStruct((27 * C, C), F32),
        ),
        in_specs=[any_space] * 8,
        out_specs=(any_space,) * 4,
        scratch_shapes=[
            vmem((C, 2 * PLANE), BF16),
            vmem((C, 2 * PLANE), BF16),
            vmem((2 * KZ, C, C), BF16),
            vmem((3, 9, C, C), BF16),
            vmem((256, PLANE), BF16),
            vmem((4, 512, 512), BF16),
            vmem((256, 256), BF16),
            vmem((16, PLANE), BF16),
            vmem((C, 2 * PLANE), BF16),
            vmem((C, 2 * PLANE), BF16),
            vmem((2 * KZ, C, C), F32),
            vmem((27 * C, C), F32),
            vmem((8, G, 16, 128), BF16),
            vmem((8, G, 16, 128), BF16),
            vmem((2, C, PLANE), BF16),
            vmem((2, C, PLANE), BF16),
            vmem((9 * C, 4 * PLANE), BF16),
            vmem((3 * C, 9 * C), BF16),
            vmem((3 * C, 9 * C), BF16),
            vmem((KZ, 128, 128), BF16),
            vmem((128, PLANE), F32),
            vmem((128, PLANE), BF16),
            vmem((256, 128), BF16),
            vmem((256, 128), BF16),
            vmem((1024, 128), BF16),
            vmem((G, 64, 128), BF16),
            vmem((64, 128), BF16),
            vmem((G, 64, 128), BF16),
            vmem((64, 128), BF16),
            vmem((G, 64, 128), BF16),
            dma((8,)),
            dma((4,)),
            dma((8, G)),
            dma((8, G)),
            dma((2, 4)),
            dma((3, G)),
            dma((3, G)),
        ],
        compiler_params=pltpu.CompilerParams(
            collective_id=0, has_side_effects=True, vmem_limit_bytes=40 << 20
        ),
    )(
        snapshots.reshape(C, 2 * PLANE),
        cotangent.reshape(C, 2 * PLANE),
        mode_weight.reshape(2 * KZ, C, C),
        conv_weight.reshape(3, 9, C, C),
        jnp.asarray(plane),
        jnp.asarray(depth),
        jnp.asarray(swap),
        jnp.asarray(inside),
    )
    activated, input_gradient, mode_gradient, conv_gradient = outs
    return (
        activated.reshape(1, C, 2, PLANE),
        input_gradient.reshape(1, C, 2, PLANE),
        mode_gradient.reshape(1, 1, 2 * KZ, C, C),
        conv_gradient.reshape(3, 3, 3, C, C),
    )


def solution(mesh):
    in_specs = (
        P("batch", None, "space", None),
        P("batch", None, "space", None),
        P("batch", "space", None, None, None),
        P(),
    )
    out_specs = in_specs
    return jax.shard_map(shards, mesh=mesh, in_specs=in_specs, out_specs=out_specs, check_vma=False)
```

time: 520 us -> 80.8 us (0.16)
  waiting for transfers between devices: 280 us -> 0 us
  local copies, waits for them, and re-layouts: 117 us -> 11.9 us
  Pallas kernels: 0 us -> 67 us
  matrix products: 47.2 us -> 0 us
  starting transfers between devices: 37.6 us -> 0 us
  other arithmetic: 17.1 us -> 0 us
  between operations: 15.2 us -> 0.67 us
    psum x1 -> x0, waiting for transfers between devices: 175 us -> none  [shards(): kernel_total = lax.psum(kernel_local, ('batch', 'space'))]
    reduce_scatter x1 -> x0, waiting for transfers between devices: 92.2 us -> none  [shards(): lax.psum_scatter(jnp.einsum('ipxy,opxy->xypio', coef, mixed_grad, preferr...]
    another operation x56 -> x0, local copies, waits for them, and re-layouts: 80.2 us -> none  [the longest x53 76.6 us: stacked_window(): jnp.stack([window[:, offset_z:offset_z + depth_cells] for offset_z in ran...]
    pallas_call x0 -> x1, Pallas kernels: none -> 67 us  [shards(): pl.pallas_call(kernel, name='layer', out_shape=(jax.ShapeDtypeStruct((C,...]
    dot_general x37 -> x0, matrix products: 47.2 us -> none  [the longest x18 22.9 us: stencil(): lax.dot_general(kernel[:, offset_x, offset_y], stacked, (((0, 1), (0, 1))...]
    all_to_all x4 -> x0, starting transfers between devices: 27.9 us -> none  [the longest x2 15.8 us: to_pencils(): lax.all_to_all(values, 'space', split_axis=3, concat_axis=1, tiled=True)]
    all_to_all x4 -> x0, waiting for transfers between devices: 11.7 us -> none  [the longest x2 8.91 us: to_pencils(): lax.all_to_all(values, 'space', split_axis=3, concat_axis=1, tiled=True)]
    slice x6 -> x0, local copies, waits for them, and re-layouts: 11.6 us -> none  [the longest x4 10.7 us: stacked_window(): window[:, offset_z:offset_z + depth_cells]]
  transfers between devices with their start and end apart: 11 -> 0, of which waited for: 5 -> 0; matrix products, arithmetic and copies ran while one was open for 30% -> 0% of each run, Pallas kernels for 0% -> 0%
where the time goes in v1:
time: 80.8 us; the launch traced here: 79.5 us
  Pallas kernels  67 us (83%)
  local copies, waits for them, and re-layouts  11.9 us (15%)
    pallas_call x1, Pallas kernels, shards(): pl.pallas_call(kernel, name='layer', out_shape=(jax.ShapeDtypeStruct((C,...  67 us
    unnamed x16, local copies, waits for them, and re-layouts  10.1 us

profile of v1, /device:TPU:1, one launch (start us, length us, event | category | flops | bytes accessed | tf_op | source)
XLA Modules:
  0.0 79.5 jit_solution(6167359970507512415)
XLA Ops:
  0.6 1.0 %copy.12 = bf16[8,8,2,1024]{3,1,2,0:T(8,128)(2,1)S(1)} copy(bf16[8,8,2,1024]{3,2,1,0:T(2,128)(2,1)} %bitcast.16) | data formatting | bytes 524288
  1.6 1.0 %copy.13 = bf16[8,8,2,1024]{3,1,2,0:T(8,128)(2,1)S(1)} copy(bf16[8,8,2,1024]{3,2,1,0:T(2,128)(2,1)} %bitcast.17) | data formatting | bytes 524288
  2.6 0.0 copy-start
  2.7 1.6 %copy-done = bf16[4,512,512]{2,1,0:T(8,128)(2,1)S(1)} copy-done((bf16[4,512,512]{2,1,0:T(8,128)(2,1)S(1)}, bf16[4,512,512]{2,1,0:T(8,128)(2,1)}, u32[]{:S(2)}) %copy-start) | copy-done | bytes 2097176
  4.2 0.0 copy-start.1
  4.2 1.0 %copy-done.1 = bf16[256,1024]{1,0:T(8,128)(2,1)S(1)} copy-done((bf16[256,1024]{1,0:T(8,128)(2,1)S(1)}, bf16[256,1024]{1,0:T(8,128)(2,1)}, u32[]{:S(2)}) %copy-start.1) | copy-done | bytes 524312
  5.3 0.0 copy-start.2
  5.3 1.0 %copy-done.2 = bf16[3,3,3,64,64]{4,3,2,1,0:T(8,128)(2,1)S(1)} copy-done((bf16[3,3,3,64,64]{4,3,2,1,0:T(8,128)(2,1)S(1)}, bf16[3,3,3,64,64]{4,3,2,1,0:T(8,128)(2,1)}, u32[]{:S(2)}) %copy-start.2) | copy-done | bytes 221208
  6.3 0.0 copy-start.3
  6.3 1.0 %copy-done.3 = bf16[1,1,24,64,64]{4,3,2,1,0:T(8,128)(2,1)S(1)} copy-done((bf16[1,1,24,64,64]{4,3,2,1,0:T(8,128)(2,1)S(1)}, bf16[1,1,24,64,64]{4,3,2,1,0:T(8,128)(2,1)}, u32[]{:S(2)}) %copy-start.3) | copy-done | bytes 196632
  7.3 0.0 copy-start.4
  7.3 0.9 %copy-done.4 = bf16[256,256]{1,0:T(8,128)(2,1)S(1)} copy-done((bf16[256,256]{1,0:T(8,128)(2,1)S(1)}, bf16[256,256]{1,0:T(8,128)(2,1)}, u32[]{:S(2)}) %copy-start.4) | copy-done | bytes 131096
  8.2 0.0 copy-start.5
  8.2 0.8 copy-done.5
  9.0 67.0 %layer.1 = (bf16[64,2048]{1,0:T(8,128)(2,1)S(1)}, bf16[64,2048]{1,0:T(8,128)(2,1)S(1)}, f32[24,64,64]{2,1,0:T(8,128)S(1)}, f32[1728,64]{1,0:T(8,128)S(1)}) custom-call(bf16[64,2048]{1,0:T(8,128)(2,1)S(1)} %bitcast.10, bf16[64,2048]{1,0:T(8,128)(2,1)S(1)} %bitcast.11, bf16[24,64,64]{2,1,0:T(8,128)(2,1)S(1)} %bitcast.15, bf16[3,9,64,64]{3,2,1,0:T(8,128)(2,1)S(1)} %bitcast.14, ...), custom_call_target="tpu_custom_call" | custom-call | tf_op jit(solution)/shard_map/layer/pallas_call | solution.py:414
  75.9 0.9 %reshape.36 = bf16[1,64,2,1024]{3,2,1,0:T(2,128)(2,1)} reshape(bf16[64,2048]{1,0:T(8,128)(2,1)S(1)} %get-tuple-element.8) | data formatting | bytes 524288 | tf_op jit(solution)/shard_map/reshape | solution.py:479
  76.8 0.9 %reshape.37 = bf16[1,64,2,1024]{3,2,1,0:T(2,128)(2,1)} reshape(bf16[64,2048]{1,0:T(8,128)(2,1)S(1)} %get-tuple-element.9) | data formatting | bytes 524288 | tf_op jit(solution)/shard_map/reshape | solution.py:480
  77.7 0.9 %copy.16 = f32[1,1,24,64,64]{4,3,2,1,0:T(8,128)} copy(f32[1,1,24,64,64]{4,3,2,1,0:T(8,128)S(1)} %bitcast.13) | data formatting | bytes 786432
  78.6 0.9 %copy.17 = f32[3,3,3,64,64]{4,3,2,1,0:T(8,128)} copy(f32[3,3,3,64,64]{4,3,2,1,0:T(8,128)S(1)} %bitcast.12) | data formatting | bytes 884736
Async XLA Ops:
  2.6 1.6 %copy-start = (bf16[4,512,512]{2,1,0:T(8,128)(2,1)S(1)}, bf16[4,512,512]{2,1,0:T(8,128)(2,1)}, u32[]{:S(2)}) copy-start(bf16[4,512,512]{2,1,0:T(8,128)(2,1)} %constant.9.clone.depth_in) | copy-start | bytes 6291460
  4.2 1.0 %copy-start.1 = (bf16[256,1024]{1,0:T(8,128)(2,1)S(1)}, bf16[256,1024]{1,0:T(8,128)(2,1)}, u32[]{:S(2)}) copy-start(bf16[256,1024]{1,0:T(8,128)(2,1)} %constant.8.clone.plane_in) | copy-start | bytes 1572868
  5.3 1.0 %copy-start.2 = (bf16[3,3,3,64,64]{4,3,2,1,0:T(8,128)(2,1)S(1)}, bf16[3,3,3,64,64]{4,3,2,1,0:T(8,128)(2,1)}, u32[]{:S(2)}) copy-start(bf16[3,3,3,64,64]{4,3,2,1,0:T(8,128)(2,1)} %param.11) | copy-start | bytes 663556
  6.3 1.0 %copy-start.3 = (bf16[1,1,24,64,64]{4,3,2,1,0:T(8,128)(2,1)S(1)}, bf16[1,1,24,64,64]{4,3,2,1,0:T(8,128)(2,1)}, u32[]{:S(2)}) copy-start(bf16[1,1,24,64,64]{4,3,2,1,0:T(8,128)(2,1)} %param.10) | copy-start | bytes 589828
  7.3 0.9 %copy-start.4 = (bf16[256,256]{1,0:T(8,128)(2,1)S(1)}, bf16[256,256]{1,0:T(8,128)(2,1)}, u32[]{:S(2)}) copy-start(bf16[256,256]{1,0:T(8,128)(2,1)} %constant.10.clone.swap_in) | copy-start | bytes 393220
  8.2 0.8 copy-start.5

commit v2 on v1

--- a/solution.py
+++ b/solution.py
@@ -79,13 +79,14 @@
     act_out, grad_out, mode_out, conv_out,
     x, cot, w, cw, plane, depth, swap, inside,
     act, grad, mode, conv,
-    send, recv, halo, pre_halo, cols, forward_w, back_w, mix_w, total, pg, coef, coef_back,
+    send, recv, halo, pre_halo, cols, forward_w, back_w, mix_w, total, pg, layers, cot_layers, act_layers, coef, coef_back,
     part_send, part_recv, term_send, term_recv, full_send, full_recv,
     in_sem, out_sem, send_sem, recv_sem, halo_sem, sum_send_sem, sum_recv_sem,
 ):
     me_b = lax.axis_index("batch")
     me_s = lax.axis_index("space")
     mine = {"batch": me_b, "space": me_s}
+    beside = me_s - me_s % 2
 
     loads = [
         pltpu.make_async_copy(source, target, in_sem.at[i])
@@ -105,9 +106,14 @@
         for axis in ("space", "batch"):
             peer = lax.rem(mine[axis] + step, G)
             pl.semaphore_signal(barrier, inc=1, device_id={axis: peer}, device_id_type=MESH)
+        across = {"batch": lax.rem(me_b + step, G), "space": beside + 1 - me_s % 2}
+        pl.semaphore_signal(barrier, inc=1, device_id=across, device_id_type=MESH)
         return carry
 
     lax.fori_loop(1, G, greet, 0)
+
+    def peer_of(axis, i):
+        return lax.rem(mine[axis] + 1 + i, G)
 
     def tile_copy(phase, axis, source, slot):
         return pltpu.make_async_remote_copy(
@@ -125,30 +131,30 @@
         recv[phase, me] = send[phase, me]
 
         def step(i, carry):
-            tile_copy(phase, axis, lax.rem(me + i, G), me).start()
+            tile_copy(phase, axis, peer_of(axis, i), me).start()
             return carry
 
-        lax.fori_loop(1, G, step, 0)
+        lax.fori_loop(0, G - 1, step, 0)
 
     def exchange_wait(phase, axis):
         me = mine[axis]
 
         def step(i, carry):
-            peer = lax.rem(me + i, G)
+            peer = peer_of(axis, i)
             tile_copy(phase, axis, peer, peer).wait_recv()
             return carry
 
-        lax.fori_loop(1, G, step, 0)
+        lax.fori_loop(0, G - 1, step, 0)
         return recv[phase].reshape(256, 128)
 
     def exchange_drain(phase, axis):
         me = mine[axis]
 
         def step(i, carry):
-            tile_copy(phase, axis, lax.rem(me + i, G), me).wait_send()
+            tile_copy(phase, axis, peer_of(axis, i), me).wait_send()
             return carry
 
-        lax.fori_loop(1, G, step, 0)
+        lax.fori_loop(0, G - 1, step, 0)
 
     def halo_copy(source, target, slot, which, offset):
         return pltpu.make_async_remote_copy(
@@ -183,22 +189,32 @@
             last = mm(weights[0:C, :], cols[:, lanes[3]])
             total[:, pl.ds(chunk * width, width)] = acc + jnp.concatenate([first, last], axis=0)
 
+    row = lax.broadcasted_iota(jnp.int32, (128, 128), 0)
+    column = lax.broadcasted_iota(jnp.int32, (128, 128), 1)
+    split = jnp.where(column == lax.rem(row, C) * 2 + row // C, 1.0, 0.0).astype(BF16)
+
+    def by_layer_of(ref):
+        return mm(split, ref[...].reshape(128, PLANE)).astype(BF16)
+
+    def by_channel_of(value):
+        return mm(split, value, 0, 0).astype(BF16).reshape(C, 2, value.shape[1])
+
     loads[0].wait()
     loads[1].wait()
-    both_layers = jnp.concatenate([x[:, :PLANE], x[:, PLANE:]], axis=0)
-    plane_coef = mm(plane[...], both_layers, 1, 1).astype(BF16)
-    pl.semaphore_wait(barrier, 2 * (G - 1))
+    layers[...] = by_layer_of(x)
+    plane_coef = mm(plane[...], layers[...], 1, 1).astype(BF16)
+    pl.semaphore_wait(barrier, 3 * (G - 1))
     exchange_start(0, "space", plane_coef)
     halos = [
-        halo_copy(x.at[:, pl.ds(PLANE, PLANE)], halo, 0, 0, 1),
-        halo_copy(x.at[:, pl.ds(0, PLANE)], halo, 1, 1, G - 1),
+        halo_copy(layers.at[pl.ds(C, C), :], halo, 0, 0, 1),
+        halo_copy(layers.at[pl.ds(0, C), :], halo, 1, 1, G - 1),
     ]
     for copy in halos:
         copy.start()
 
     loads[2].wait()
     loads[3].wait()
-    spread(1, x[:, :PLANE])
+    spread(1, layers[:C, :])
     tiles = exchange_wait(0, "space")
     exchange_start(1, "batch", depth_transform(0, tiles))
 
@@ -230,7 +246,7 @@
     mixed = [mm(coef[rows_of(p), :], mix_w[p]) for p in range(KZ)]
     exchange_start(2, "batch", pad_and_swap(mixed))
 
-    spread(2, x[:, PLANE:])
+    spread(2, layers[C:, :])
     for copy in halos:
         copy.wait_recv()
     spread(0, jnp.where(me_s > 0, halo[0], jnp.zeros_like(halo[0])))
@@ -240,6 +256,7 @@
     exchange_start(3, "space", depth_transform(1, tiles))
     stencil(forward_w)
     loads[7].wait()
+    cot_layers[...] = by_layer_of(cot)
     tiles = exchange_wait(3, "space")
     doubled = tiles * jnp.asarray(2.0, BF16)
 
@@ -249,18 +266,14 @@
     for layer in range(2):
         for chunk in range(4):
             lanes = pl.ds(chunk * 256, 256)
-            cells = pl.ds(layer * PLANE + chunk * 256, 256)
             rows = pl.ds(layer * C, C)
             pre = total[rows, lanes]
             normal_cdf = 0.5 * (1.0 + lax.erf(pre * inv_root_two))
             density = jnp.exp(-0.5 * pre * pre) * inv_root_two_pi
-            act[:, cells] = (pre * normal_cdf).astype(BF16)
+            act_layers[rows, lanes] = (pre * normal_cdf).astype(BF16)
             pg[rows, lanes] = (
-                cot[:, cells].astype(F32) * (normal_cdf + pre * density)
+                cot_layers[rows, lanes].astype(F32) * (normal_cdf + pre * density)
             ).astype(BF16)
-    stores = [pltpu.make_async_copy(act, act_out, out_sem.at[0])]
-    stores[0].start()
-
     back_plane = (mm(plane[...], pg[...], 1, 1) * 2.0).astype(BF16)
     exchange_start(4, "space", back_plane)
     pre_halos = [
@@ -269,6 +282,12 @@
     ]
     for copy in pre_halos:
         copy.start()
+
+    for chunk in range(4):
+        lanes = pl.ds(chunk * 256, 256)
+        act[:, :, lanes] = by_channel_of(act_layers[:, lanes])
+    stores = [pltpu.make_async_copy(act, act_out, out_sem.at[0])]
+    stores[0].start()
 
     for r in range(3):
         rows = pl.ds(r * 192, 192)
@@ -282,70 +301,68 @@
         ).astype(BF16)
     part_send[pl.ds(864, 160), :] = jnp.zeros((160, 128), BF16)
 
-    def sum_copy(stage, axis, source, target, peer, slot):
+    def part_rows(i):
+        return part_send.at[pl.ds(pl.multiple_of(i * 32, 32), 32), :]
+
+    def in_layer(i):
+        return {"batch": i // 2, "space": beside + i % 2}
+
+    def in_column(i):
+        return {"space": i * 2 + me_s % 2}
+
+    at_layer = me_b * 2 + me_s % 2
+    stages = (
+        (32, at_layer, in_layer, part_rows, part_recv),
+        (8, me_s // 2, in_column, lambda i: term_send, term_recv),
+        (32, at_layer, in_layer, lambda i: full_send, full_recv),
+    )
+
+    def sum_loop(stage, act_on):
+        count, me, device, source, target = stages[stage]
+
+        def step(i, carry):
+            peer = lax.rem(me + i, count)
+            act_on(peer, me, device, source, target)
+            return carry
+
+        lax.fori_loop(1, count, step, 0)
+
+    def sum_copy(stage, peer, slot, device, source, target):
         return pltpu.make_async_remote_copy(
-            src_ref=source,
+            src_ref=source(peer),
             dst_ref=target.at[slot],
             send_sem=sum_send_sem.at[stage, peer],
             recv_sem=sum_recv_sem.at[stage, slot],
-            device_id={axis: peer},
+            device_id=device(peer),
             device_id_type=MESH,
         )
 
-    def part_rows(i):
-        return part_send.at[pl.ds(pl.multiple_of(i * 64, 64), 64), :]
-
-    stages = (
-        ("space", part_rows, part_recv),
-        ("batch", lambda i: term_send, term_recv),
-        ("space", lambda i: full_send, full_recv),
-    )
-
     def sum_start(stage):
-        axis, source, target = stages[stage]
-        me = mine[axis]
+        count, me, device, source, target = stages[stage]
         target[me] = source(me)[...]
-
-        def step(i, carry):
-            peer = lax.rem(me + i, G)
-            sum_copy(stage, axis, source(peer), target, peer, me).start()
-            return carry
-
-        lax.fori_loop(1, G, step, 0)
+        sum_loop(stage, lambda peer, me, *rest: sum_copy(stage, peer, me, *rest).start())
 
     def sum_wait(stage):
-        axis, source, target = stages[stage]
-        me = mine[axis]
-
-        def step(i, carry):
-            peer = lax.rem(me + i, G)
-            sum_copy(stage, axis, source(peer), target, peer, peer).wait_recv()
-            return carry
-
-        lax.fori_loop(1, G, step, 0)
+        sum_loop(stage, lambda peer, me, *rest: sum_copy(stage, peer, peer, *rest).wait_recv())
 
     def sum_drain(stage):
-        axis, source, target = stages[stage]
-        me = mine[axis]
-
-        def step(i, carry):
-            peer = lax.rem(me + i, G)
-            sum_copy(stage, axis, source(peer), target, peer, me).wait_send()
-            return carry
-
-        lax.fori_loop(1, G, step, 0)
+        sum_loop(stage, lambda peer, me, *rest: sum_copy(stage, peer, me, *rest).wait_send())
 
     def added(target):
         value = target[0].astype(F32)
-        for i in range(1, G):
+        for i in range(1, target.shape[0]):
             value = value + target[i].astype(F32)
         return value
 
+    sum_start(0)
     tiles = exchange_wait(4, "space")
     exchange_start(5, "batch", depth_transform(2, tiles))
-    sum_start(0)
 
     spread(1, pg[:C, :])
+    spread(2, pg[C:, :])
+    sum_wait(0)
+    term_send[...] = added(part_recv).astype(BF16)
+    sum_start(1)
     tiles = exchange_wait(5, "batch")
     coef_back[...] = mm(swap[...], tiles).astype(BF16)
     gradients = [mm(coef_back[rows_of(p), :], mix_w[p], 1, 1) for p in range(KZ)]
@@ -358,11 +375,9 @@
     stores.append(pltpu.make_async_copy(mode, mode_out, out_sem.at[1]))
     stores[1].start()
 
-    spread(2, pg[C:, :])
-    sum_wait(0)
-    term_send[...] = added(part_recv).astype(BF16)
-    sum_start(1)
-
+    sum_wait(1)
+    full_send[...] = (added(term_recv) * conv_scale).astype(BF16)
+    sum_start(2)
     tiles = exchange_wait(6, "batch")
     exchange_start(7, "space", depth_transform(3, tiles))
 
@@ -370,29 +385,25 @@
         copy.wait_recv()
     spread(0, jnp.where(me_s > 0, pre_halo[0], jnp.zeros_like(pre_halo[0])))
     spread(3, jnp.where(me_s < G - 1, pre_halo[1], jnp.zeros_like(pre_halo[1])))
-    sum_wait(1)
-    full_send[...] = (added(term_recv) * conv_scale).astype(BF16)
-    sum_start(2)
     stencil(back_w)
 
     tiles = exchange_wait(7, "space")
     for chunk in range(4):
         lanes = pl.ds(chunk * 256, 256)
         value = (total[:, lanes] + mm(tiles, plane[:, lanes], 0, 0)).astype(BF16)
-        grad[:, lanes] = value[:C]
-        grad[:, pl.ds(PLANE + chunk * 256, 256)] = value[C:]
+        grad[:, :, lanes] = by_channel_of(value)
     stores.append(pltpu.make_async_copy(grad, grad_out, out_sem.at[2]))
     stores[2].start()
 
     sum_wait(2)
     for i in range(9):
-        value = full_recv[i].astype(F32)
+        value = full_recv[2 * i : 2 * i + 2].reshape(64, 128).astype(F32)
         conv[pl.ds(i * 64, 64), :] = value[:, :C]
         conv[pl.ds(576 + i * 64, 64), :] = value[:, C:]
-    rest = full_recv[9:14].reshape(320, 128).astype(F32)
     for r in range(3):
-        conv[pl.ds(1152 + r * 192, 96), :] = rest[r * 96 : (r + 1) * 96, :C]
-        conv[pl.ds(1152 + r * 192 + 96, 96), :] = rest[r * 96 : (r + 1) * 96, C:]
+        value = full_recv[18 + 3 * r : 21 + 3 * r].reshape(96, 128).astype(F32)
+        conv[pl.ds(1152 + r * 192, 96), :] = value[:, :C]
+        conv[pl.ds(1152 + r * 192 + 96, 96), :] = value[:, C:]
     stores.append(pltpu.make_async_copy(conv, conv_out, out_sem.at[3]))
     stores[3].start()
 
@@ -406,33 +417,46 @@
         store.wait()
 
 
+def deliver(*refs):
+    sources, targets, held, (in_sem, out_sem) = refs[:4], refs[4:8], refs[8:12], refs[12:]
+    loads = [pltpu.make_async_copy(sources[i], held[i], in_sem.at[i]) for i in range(4)]
+    stores = [pltpu.make_async_copy(held[i], targets[i], out_sem.at[i]) for i in range(4)]
+    for load in loads:
+        load.start()
+    for load, store in zip(loads, stores):
+        load.wait()
+        store.start()
+    for store in stores:
+        store.wait()
+
+
 def shards(snapshots, cotangent, mode_weight, conv_weight):
     plane, depth, swap, inside = make_tables()
-    any_space = pl.BlockSpec(memory_space=pl.ANY)
+    any_space = pl.BlockSpec(memory_space=pltpu.HBM)
     vmem = pltpu.VMEM
     dma = pltpu.SemaphoreType.DMA
     outs = pl.pallas_call(
         kernel,
         name="layer",
         out_shape=(
-            jax.ShapeDtypeStruct((C, 2 * PLANE), BF16),
-            jax.ShapeDtypeStruct((C, 2 * PLANE), BF16),
+            jax.ShapeDtypeStruct((C, 2, PLANE), BF16),
+            jax.ShapeDtypeStruct((C, 2, PLANE), BF16),
             jax.ShapeDtypeStruct((2 * KZ, C, C), F32),
             jax.ShapeDtypeStruct((27 * C, C), F32),
         ),
         in_specs=[any_space] * 8,
         out_specs=(any_space,) * 4,
         scratch_shapes=[
-            vmem((C, 2 * PLANE), BF16),
-            vmem((C, 2 * PLANE), BF16),
+            vmem((C, 2, PLANE), BF16),
+            vmem((C, 2, PLANE), BF16),
             vmem((2 * KZ, C, C), BF16),
             vmem((3, 9, C, C), BF16),
             vmem((256, PLANE), BF16),
             vmem((4, 512, 512), BF16),
             vmem((256, 256), BF16),
             vmem((16, PLANE), BF16),
-            vmem((C, 2 * PLANE), BF16),
-            vmem((C, 2 * PLANE), BF16),
+            vmem((C, 2, PLANE), BF16),
+            vmem((C, 2, PLANE), BF16),
             vmem((2 * KZ, C, C), F32),
             vmem((27 * C, C), F32),
             vmem((8, G, 16, 128), BF16),
@@ -445,28 +469,31 @@
             vmem((KZ, 128, 128), BF16),
             vmem((128, PLANE), F32),
             vmem((128, PLANE), BF16),
+            vmem((128, PLANE), BF16),
+            vmem((128, PLANE), BF16),
+            vmem((128, PLANE), BF16),
             vmem((256, 128), BF16),
             vmem((256, 128), BF16),
             vmem((1024, 128), BF16),
-            vmem((G, 64, 128), BF16),
-            vmem((64, 128), BF16),
-            vmem((G, 64, 128), BF16),
-            vmem((64, 128), BF16),
-            vmem((G, 64, 128), BF16),
+            vmem((32, 32, 128), BF16),
+            vmem((32, 128), BF16),
+            vmem((8, 32, 128), BF16),
+            vmem((32, 128), BF16),
+            vmem((32, 32, 128), BF16),
             dma((8,)),
             dma((4,)),
             dma((8, G)),
             dma((8, G)),
             dma((2, 4)),
-            dma((3, G)),
-            dma((3, G)),
+            dma((3, 32)),
+            dma((3, 32)),
         ],
         compiler_params=pltpu.CompilerParams(
-            collective_id=0, has_side_effects=True, vmem_limit_bytes=40 << 20
+            collective_id=0, has_side_effects=True, vmem_limit_bytes=60 << 20
         ),
     )(
-        snapshots.reshape(C, 2 * PLANE),
-        cotangent.reshape(C, 2 * PLANE),
+        snapshots[0],
+        cotangent[0],
         mode_weight.reshape(2 * KZ, C, C),
         conv_weight.reshape(3, 9, C, C),
         jnp.asarray(plane),
@@ -474,6 +501,15 @@
         jnp.asarray(swap),
         jnp.asarray(inside),
     )
+    outs = pl.pallas_call(
+        deliver,
+        name="deliver",
+        out_shape=tuple(jax.ShapeDtypeStruct(out.shape, out.dtype) for out in outs),
+        in_specs=[any_space] * 4,
+        out_specs=(any_space,) * 4,
+        scratch_shapes=[vmem(out.shape, out.dtype) for out in outs] + [dma((4,)), dma((4,))],
+        compiler_params=pltpu.CompilerParams(vmem_limit_bytes=60 << 20),
+    )(*outs)
     activated, input_gradient, mode_gradient, conv_gradient = outs
     return (
         activated.reshape(1, C, 2, PLANE),

time: 80.8 us -> 67.1 us (0.83); the launches traced: 79.5 us -> 67 us
  local copies, waits for them, and re-layouts: 11.9 us -> 0 us
    unnamed x16 -> x0, local copies, waits for them, and re-layouts: 10.1 us -> none
    pallas_call x1, Pallas kernels: 67 us -> 63.8 us  [shards(): pl.pallas_call(kernel, name='layer', out_shape=(jax.ShapeDtypeStruct((C,...]
    pallas_call x0 -> x1, Pallas kernels: none -> 2.55 us  [shards(): pl.pallas_call(deliver, name='deliver', out_shape=tuple((jax.ShapeDtypeSt...]
    reshape x2 -> x0, local copies, waits for them, and re-layouts: 1.76 us -> none  [the longest x1 0.88 us: shards(): activated.reshape(1, C, 2, PLANE)]
where the time goes in v2:
time: 67.1 us; the launch traced here: 67 us
  Pallas kernels  66.4 us (99%)
    pallas_call x1, Pallas kernels, shards(): pl.pallas_call(kernel, name='layer', out_shape=(jax.ShapeDtypeStruct((C,...  63.8 us
    pallas_call x1, Pallas kernels, shards(): pl.pallas_call(deliver, name='deliver', out_shape=tuple((jax.ShapeDtypeSt...  2.55 us

profile of v2, /device:TPU:1, one launch (start us, length us, event | category | flops | bytes accessed | tf_op | source)
XLA Modules:
  0.0 67.0 jit_solution(2779034665218591862)
XLA Ops:
  0.6 63.8 %layer.1 = (bf16[64,2,1024]{2,1,0:T(2,128)(2,1)}, bf16[64,2,1024]{2,1,0:T(2,128)(2,1)}, f32[24,64,64]{2,1,0:T(8,128)}, f32[1728,64]{1,0:T(8,128)}) custom-call(bf16[64,2,1024]{2,1,0:T(2,128)(2,1)} %bitcast.10, bf16[64,2,1024]{2,1,0:T(2,128)(2,1)} %bitcast.11, bf16[24,64,64]{2,1,0:T(8,128)(2,1)} %bitcast.9, bf16[3,9,64,64]{3,2,1,0:T(8,128)(2,1)} %bitcast.8, ...), custom_call_target="tpu_custom_call" | custom-call | tf_op jit(solution)/shard_map/layer/pallas_call | solution.py:438
  64.5 2.6 %deliver.1 = (bf16[64,2,1024]{2,1,0:T(2,128)(2,1)}, bf16[64,2,1024]{2,1,0:T(2,128)(2,1)}, f32[24,64,64]{2,1,0:T(8,128)}, f32[1728,64]{1,0:T(8,128)}) custom-call(bf16[64,2,1024]{2,1,0:T(2,128)(2,1)} %get-tuple-element.12.refs_0_, bf16[64,2,1024]{2,1,0:T(2,128)(2,1)} %get-tuple-element.13.refs_1_, f32[24,64,64]{2,1,0:T(8,128)} %get-tuple-element.14.refs_2_, ...), custom_call_target="tpu_custom_call" | custom-call | tf_op jit(solution)/shard_map/deliver/pallas_call | solution.py:504

commit v3 on v2

--- a/solution.py
+++ b/solution.py
@@ -79,7 +79,7 @@
     act_out, grad_out, mode_out, conv_out,
     x, cot, w, cw, plane, depth, swap, inside,
     act, grad, mode, conv,
-    send, recv, halo, pre_halo, cols, forward_w, back_w, mix_w, total, pg, layers, cot_layers, act_layers, coef, coef_back,
+    send, recv, halo, pre_halo, cols, forward_w, back_w, mix_w, unmix_w, total, pg, layers, cot_layers, act_layers, coef, coef_back,
     part_send, part_recv, term_send, term_recv, full_send, full_recv,
     in_sem, out_sem, send_sem, recv_sem, halo_sem, sum_send_sem, sum_recv_sem,
 ):
@@ -119,8 +119,8 @@
         return pltpu.make_async_remote_copy(
             src_ref=send.at[phase, source],
             dst_ref=recv.at[phase, slot],
-            send_sem=send_sem.at[phase, source],
-            recv_sem=recv_sem.at[phase, slot],
+            send_sem=send_sem.at[phase],
+            recv_sem=recv_sem.at[phase],
             device_id={axis: source},
             device_id_type=MESH,
         )
@@ -136,25 +136,16 @@
 
         lax.fori_loop(0, G - 1, step, 0)
 
-    def exchange_wait(phase, axis):
-        me = mine[axis]
-
-        def step(i, carry):
-            peer = peer_of(axis, i)
-            tile_copy(phase, axis, peer, peer).wait_recv()
-            return carry
-
-        lax.fori_loop(0, G - 1, step, 0)
+    def all_bytes(buffer, sem):
+        others = buffer.at[pl.ds(0, buffer.shape[0] - 1)]
+        pltpu.make_async_copy(others, others, sem).wait()
+
+    def exchange_wait(phase):
+        all_bytes(recv.at[phase], recv_sem.at[phase])
         return recv[phase].reshape(256, 128)
 
-    def exchange_drain(phase, axis):
-        me = mine[axis]
-
-        def step(i, carry):
-            tile_copy(phase, axis, peer_of(axis, i), me).wait_send()
-            return carry
-
-        lax.fori_loop(0, G - 1, step, 0)
+    def exchange_drain(phase):
+        all_bytes(send.at[phase], send_sem.at[phase])
 
     def halo_copy(source, target, slot, which, offset):
         return pltpu.make_async_remote_copy(
@@ -215,7 +206,7 @@
     loads[2].wait()
     loads[3].wait()
     spread(1, layers[:C, :])
-    tiles = exchange_wait(0, "space")
+    tiles = exchange_wait(0)
     exchange_start(1, "batch", depth_transform(0, tiles))
 
     loads[4].wait()
@@ -233,18 +224,19 @@
         mix_w[p, :C, :C] = w[p]
         mix_w[p, C:, C:] = w[KZ + p]
 
-    tiles = exchange_wait(1, "batch")
+    z_mode = lax.broadcasted_iota(jnp.int32, (256, 128), 0) % 16
+
+    def mix(tiles, weights):
+        picked = [
+            tiles * jnp.where(z_mode == p, 1.0, 0.0).astype(BF16) for p in range(KZ)
+        ]
+        return mm(jnp.concatenate(picked, axis=1), weights[...].reshape(KZ * 128, 128)).astype(BF16)
+
+    tiles = exchange_wait(1)
+    exchange_start(2, "batch", mix(tiles, mix_w))
     coef[...] = mm(swap[...], tiles).astype(BF16)
-
-    def rows_of(p):
-        return pl.ds(p * 16, 16)
-
-    def pad_and_swap(pieces):
-        value = jnp.concatenate(pieces + [jnp.zeros((64, 128), F32)], axis=0).astype(BF16)
-        return mm(swap[...], value).astype(BF16)
-
-    mixed = [mm(coef[rows_of(p), :], mix_w[p]) for p in range(KZ)]
-    exchange_start(2, "batch", pad_and_swap(mixed))
+    for p in range(KZ):
+        unmix_w[p] = mix_w[p].astype(F32).T.astype(BF16)
 
     spread(2, layers[C:, :])
     for copy in halos:
@@ -252,12 +244,12 @@
     spread(0, jnp.where(me_s > 0, halo[0], jnp.zeros_like(halo[0])))
     spread(3, jnp.where(me_s < G - 1, halo[1], jnp.zeros_like(halo[1])))
 
-    tiles = exchange_wait(2, "batch")
+    tiles = exchange_wait(2)
     exchange_start(3, "space", depth_transform(1, tiles))
     stencil(forward_w)
     loads[7].wait()
     cot_layers[...] = by_layer_of(cot)
-    tiles = exchange_wait(3, "space")
+    tiles = exchange_wait(3)
     doubled = tiles * jnp.asarray(2.0, BF16)
 
     for chunk in range(4):
@@ -317,36 +309,29 @@
         (32, at_layer, in_layer, lambda i: full_send, full_recv),
     )
 
-    def sum_loop(stage, act_on):
-        count, me, device, source, target = stages[stage]
-
-        def step(i, carry):
-            peer = lax.rem(me + i, count)
-            act_on(peer, me, device, source, target)
-            return carry
-
-        lax.fori_loop(1, count, step, 0)
-
-    def sum_copy(stage, peer, slot, device, source, target):
-        return pltpu.make_async_remote_copy(
-            src_ref=source(peer),
-            dst_ref=target.at[slot],
-            send_sem=sum_send_sem.at[stage, peer],
-            recv_sem=sum_recv_sem.at[stage, slot],
-            device_id=device(peer),
-            device_id_type=MESH,
-        )
-
     def sum_start(stage):
         count, me, device, source, target = stages[stage]
         target[me] = source(me)[...]
-        sum_loop(stage, lambda peer, me, *rest: sum_copy(stage, peer, me, *rest).start())
+
+        def step(i, carry):
+            peer = lax.rem(me + i, count)
+            pltpu.make_async_remote_copy(
+                src_ref=source(peer),
+                dst_ref=target.at[me],
+                send_sem=sum_send_sem.at[stage],
+                recv_sem=sum_recv_sem.at[stage],
+                device_id=device(peer),
+                device_id_type=MESH,
+            ).start()
+            return carry
+
+        lax.fori_loop(1, count, step, 0)
 
     def sum_wait(stage):
-        sum_loop(stage, lambda peer, me, *rest: sum_copy(stage, peer, peer, *rest).wait_recv())
+        all_bytes(stages[stage][4], sum_recv_sem.at[stage])
 
     def sum_drain(stage):
-        sum_loop(stage, lambda peer, me, *rest: sum_copy(stage, peer, me, *rest).wait_send())
+        all_bytes(stages[stage][4], sum_send_sem.at[stage])
 
     def added(target):
         value = target[0].astype(F32)
@@ -355,7 +340,7 @@
         return value
 
     sum_start(0)
-    tiles = exchange_wait(4, "space")
+    tiles = exchange_wait(4)
     exchange_start(5, "batch", depth_transform(2, tiles))
 
     spread(1, pg[:C, :])
@@ -363,10 +348,13 @@
     sum_wait(0)
     term_send[...] = added(part_recv).astype(BF16)
     sum_start(1)
-    tiles = exchange_wait(5, "batch")
+    tiles = exchange_wait(5)
+    exchange_start(6, "batch", mix(tiles, unmix_w))
+
     coef_back[...] = mm(swap[...], tiles).astype(BF16)
-    gradients = [mm(coef_back[rows_of(p), :], mix_w[p], 1, 1) for p in range(KZ)]
-    exchange_start(6, "batch", pad_and_swap(gradients))
+
+    def rows_of(p):
+        return pl.ds(p * 16, 16)
 
     for p in range(KZ):
         product = mm(coef[rows_of(p), :], coef_back[rows_of(p), :], 0, 0)
@@ -378,7 +366,7 @@
     sum_wait(1)
     full_send[...] = (added(term_recv) * conv_scale).astype(BF16)
     sum_start(2)
-    tiles = exchange_wait(6, "batch")
+    tiles = exchange_wait(6)
     exchange_start(7, "space", depth_transform(3, tiles))
 
     for copy in pre_halos:
@@ -387,7 +375,7 @@
     spread(3, jnp.where(me_s < G - 1, pre_halo[1], jnp.zeros_like(pre_halo[1])))
     stencil(back_w)
 
-    tiles = exchange_wait(7, "space")
+    tiles = exchange_wait(7)
     for chunk in range(4):
         lanes = pl.ds(chunk * 256, 256)
         value = (total[:, lanes] + mm(tiles, plane[:, lanes], 0, 0)).astype(BF16)
@@ -407,8 +395,8 @@
     stores.append(pltpu.make_async_copy(conv, conv_out, out_sem.at[3]))
     stores[3].start()
 
-    for phase, axis in enumerate(("space", "batch", "batch", "space") * 2):
-        exchange_drain(phase, axis)
+    for phase in range(8):
+        exchange_drain(phase)
     for stage in range(3):
         sum_drain(stage)
     for copy in halos + pre_halos:
@@ -467,6 +455,7 @@
             vmem((3 * C, 9 * C), BF16),
             vmem((3 * C, 9 * C), BF16),
             vmem((KZ, 128, 128), BF16),
+            vmem((KZ, 128, 128), BF16),
             vmem((128, PLANE), F32),
             vmem((128, PLANE), BF16),
             vmem((128, PLANE), BF16),
@@ -482,11 +471,11 @@
             vmem((32, 32, 128), BF16),
             dma((8,)),
             dma((4,)),
-            dma((8, G)),
-            dma((8, G)),
+            dma((8,)),
+            dma((8,)),
             dma((2, 4)),
-            dma((3, 32)),
-            dma((3, 32)),
+            dma((3,)),
+            dma((3,)),
         ],
         compiler_params=pltpu.CompilerParams(
             collective_id=0, has_side_effects=True, vmem_limit_bytes=60 << 20

time: 67.1 us -> 61.4 us (0.915)
  Pallas kernels: 66.4 us -> 60.5 us
    pallas_call x1, Pallas kernels: 63.8 us -> 57.9 us  [shards(): pl.pallas_call(kernel, name='layer', out_shape=(jax.ShapeDtypeStruct((C,...]
where the time goes in v3:
time: 61.4 us; the launch traced here: 61.1 us
  Pallas kernels  60.5 us (99%)
  between operations  0.64 us (1%)
    pallas_call x1, Pallas kernels, shards(): pl.pallas_call(kernel, name='layer', out_shape=(jax.ShapeDtypeStruct((C,...  57.9 us
    pallas_call x1, Pallas kernels, shards(): pl.pallas_call(deliver, name='deliver', out_shape=tuple((jax.ShapeDtypeSt...  2.55 us

profile of v3, /device:TPU:1, one launch (start us, length us, event | category | flops | bytes accessed | tf_op | source)
XLA Modules:
  0.0 61.1 jit_solution(3986150710106201078)
XLA Ops:
  0.6 57.9 %layer.1 = (bf16[64,2,1024]{2,1,0:T(2,128)(2,1)}, bf16[64,2,1024]{2,1,0:T(2,128)(2,1)}, f32[24,64,64]{2,1,0:T(8,128)}, f32[1728,64]{1,0:T(8,128)}) custom-call(bf16[64,2,1024]{2,1,0:T(2,128)(2,1)} %bitcast.10, bf16[64,2,1024]{2,1,0:T(2,128)(2,1)} %bitcast.11, bf16[24,64,64]{2,1,0:T(8,128)(2,1)} %bitcast.9, bf16[3,9,64,64]{3,2,1,0:T(8,128)(2,1)} %bitcast.8, ...), custom_call_target="tpu_custom_call" | custom-call | tf_op jit(solution)/shard_map/layer/pallas_call | solution.py:426
  58.6 2.6 %deliver.1 = (bf16[64,2,1024]{2,1,0:T(2,128)(2,1)}, bf16[64,2,1024]{2,1,0:T(2,128)(2,1)}, f32[24,64,64]{2,1,0:T(8,128)}, f32[1728,64]{1,0:T(8,128)}) custom-call(bf16[64,2,1024]{2,1,0:T(2,128)(2,1)} %get-tuple-element.12.refs_0_, bf16[64,2,1024]{2,1,0:T(2,128)(2,1)} %get-tuple-element.13.refs_1_, f32[24,64,64]{2,1,0:T(8,128)} %get-tuple-element.14.refs_2_, ...), custom_call_target="tpu_custom_call" | custom-call | tf_op jit(solution)/shard_map/deliver/pallas_call | solution.py:493

commit v4 on v3

--- a/solution.py
+++ b/solution.py
@@ -78,7 +78,7 @@
     x_in, cot_in, w_in, cw_in, plane_in, depth_in, swap_in, inside_in,
     act_out, grad_out, mode_out, conv_out,
     x, cot, w, cw, plane, depth, swap, inside,
-    act, grad, mode, conv,
+    act, grad, mode,
     send, recv, halo, pre_halo, cols, forward_w, back_w, mix_w, unmix_w, total, pg, layers, cot_layers, act_layers, coef, coef_back,
     part_send, part_recv, term_send, term_recv, full_send, full_recv,
     in_sem, out_sem, send_sem, recv_sem, halo_sem, sum_send_sem, sum_recv_sem,
@@ -87,6 +87,14 @@
     me_s = lax.axis_index("space")
     mine = {"batch": me_b, "space": me_s}
     beside = me_s - me_s % 2
+
+    barrier = pltpu.get_barrier_semaphore()
+    for step in (8, 7, 9, 6, 10, 5, 11, 4, 12, 3, 13, 2, 14, 1, 15):
+        peer_b, peer_s = lax.rem(me_b + step, G), lax.rem(me_s + step, G)
+        for target in (
+            {"space": peer_s}, {"batch": peer_b}, {"batch": peer_b, "space": beside + 1 - me_s % 2},
+        ):
+            pl.semaphore_signal(barrier, inc=1, device_id=target, device_id_type=MESH)
 
     loads = [
         pltpu.make_async_copy(source, target, in_sem.at[i])
@@ -100,18 +108,6 @@
     for load in loads:
         load.start()
 
-    barrier = pltpu.get_barrier_semaphore()
-
-    def greet(step, carry):
-        for axis in ("space", "batch"):
-            peer = lax.rem(mine[axis] + step, G)
-            pl.semaphore_signal(barrier, inc=1, device_id={axis: peer}, device_id_type=MESH)
-        across = {"batch": lax.rem(me_b + step, G), "space": beside + 1 - me_s % 2}
-        pl.semaphore_signal(barrier, inc=1, device_id=across, device_id_type=MESH)
-        return carry
-
-    lax.fori_loop(1, G, greet, 0)
-
     def peer_of(axis, i):
         return lax.rem(mine[axis] + 1 + i, G)
 
@@ -128,13 +124,13 @@
     def exchange_start(phase, axis, value):
         me = mine[axis]
         send[phase] = value.reshape(G, 16, 128)
-        recv[phase, me] = send[phase, me]
 
         def step(i, carry):
             tile_copy(phase, axis, peer_of(axis, i), me).start()
             return carry
 
         lax.fori_loop(0, G - 1, step, 0)
+        recv[phase, me] = send[phase, me]
 
     def all_bytes(buffer, sem):
         others = buffer.at[pl.ds(0, buffer.shape[0] - 1)]
@@ -200,14 +196,14 @@
         halo_copy(layers.at[pl.ds(C, C), :], halo, 0, 0, 1),
         halo_copy(layers.at[pl.ds(0, C), :], halo, 1, 1, G - 1),
     ]
-    for copy in halos:
-        copy.start()
+    halos[0].start()
 
     loads[2].wait()
     loads[3].wait()
     spread(1, layers[:C, :])
     tiles = exchange_wait(0)
     exchange_start(1, "batch", depth_transform(0, tiles))
+    halos[1].start()
 
     loads[4].wait()
     for a in range(3):
@@ -272,14 +268,7 @@
         halo_copy(pg.at[pl.ds(C, C), :], pre_halo, 0, 2, 1),
         halo_copy(pg.at[pl.ds(0, C), :], pre_halo, 1, 3, G - 1),
     ]
-    for copy in pre_halos:
-        copy.start()
-
-    for chunk in range(4):
-        lanes = pl.ds(chunk * 256, 256)
-        act[:, :, lanes] = by_channel_of(act_layers[:, lanes])
-    stores = [pltpu.make_async_copy(act, act_out, out_sem.at[0])]
-    stores[0].start()
+    pre_halos[0].start()
 
     for r in range(3):
         rows = pl.ds(r * 192, 192)
@@ -342,12 +331,19 @@
     sum_start(0)
     tiles = exchange_wait(4)
     exchange_start(5, "batch", depth_transform(2, tiles))
+    pre_halos[1].start()
 
     spread(1, pg[:C, :])
-    spread(2, pg[C:, :])
     sum_wait(0)
     term_send[...] = added(part_recv).astype(BF16)
     sum_start(1)
+    spread(2, pg[C:, :])
+    for chunk in range(4):
+        lanes = pl.ds(chunk * 256, 256)
+        act[:, :, lanes] = by_channel_of(act_layers[:, lanes])
+    stores = [pltpu.make_async_copy(act, act_out, out_sem.at[0])]
+    stores[0].start()
+
     tiles = exchange_wait(5)
     exchange_start(6, "batch", mix(tiles, unmix_w))
 
@@ -356,10 +352,10 @@
     def rows_of(p):
         return pl.ds(p * 16, 16)
 
+    first_half = lax.broadcasted_iota(jnp.int32, (C, 128), 1) < C
     for p in range(KZ):
         product = mm(coef[rows_of(p), :], coef_back[rows_of(p), :], 0, 0)
-        mode[p] = product[:C, :C]
-        mode[KZ + p] = product[C:, C:]
+        mode[p] = jnp.where(first_half, product[:C], product[C:])
     stores.append(pltpu.make_async_copy(mode, mode_out, out_sem.at[1]))
     stores[1].start()
 
@@ -374,6 +370,12 @@
     spread(0, jnp.where(me_s > 0, pre_halo[0], jnp.zeros_like(pre_halo[0])))
     spread(3, jnp.where(me_s < G - 1, pre_halo[1], jnp.zeros_like(pre_halo[1])))
     stencil(back_w)
+    for phase in range(7):
+        exchange_drain(phase)
+    for stage in range(2):
+        sum_drain(stage)
+    for copy in halos + pre_halos:
+        copy.wait_send()
 
     tiles = exchange_wait(7)
     for chunk in range(4):
@@ -384,36 +386,43 @@
     stores[2].start()
 
     sum_wait(2)
+    stores.append(pltpu.make_async_copy(full_recv, conv_out, out_sem.at[3]))
+    stores[3].start()
+
+    exchange_drain(7)
+    sum_drain(2)
+    for store in stores:
+        store.wait()
+
+
+def deliver(
+    act_in, grad_in, mode_in, conv_in, act_out, grad_out, mode_out, conv_out,
+    act, grad, packed_mode, packed_conv, mode, conv, in_sem, out_sem,
+):
+    held = ((act_in, act), (grad_in, grad), (mode_in, packed_mode), (conv_in, packed_conv))
+    loads = [pltpu.make_async_copy(*pair, in_sem.at[i]) for i, pair in enumerate(held)]
+    kept = ((act, act_out), (grad, grad_out), (mode, mode_out), (conv, conv_out))
+    stores = [pltpu.make_async_copy(*pair, out_sem.at[i]) for i, pair in enumerate(kept)]
+    for i in (2, 3, 0, 1):
+        loads[i].start()
+    loads[2].wait()
+    for p in range(KZ):
+        mode[p] = packed_mode[p][:, :C]
+        mode[KZ + p] = packed_mode[p][:, C:]
+    stores[2].start()
+    loads[3].wait()
     for i in range(9):
-        value = full_recv[2 * i : 2 * i + 2].reshape(64, 128).astype(F32)
+        value = packed_conv[2 * i : 2 * i + 2].reshape(64, 128).astype(F32)
         conv[pl.ds(i * 64, 64), :] = value[:, :C]
         conv[pl.ds(576 + i * 64, 64), :] = value[:, C:]
     for r in range(3):
-        value = full_recv[18 + 3 * r : 21 + 3 * r].reshape(96, 128).astype(F32)
+        value = packed_conv[18 + 3 * r : 21 + 3 * r].reshape(96, 128).astype(F32)
         conv[pl.ds(1152 + r * 192, 96), :] = value[:, :C]
         conv[pl.ds(1152 + r * 192 + 96, 96), :] = value[:, C:]
-    stores.append(pltpu.make_async_copy(conv, conv_out, out_sem.at[3]))
     stores[3].start()
-
-    for phase in range(8):
-        exchange_drain(phase)
-    for stage in range(3):
-        sum_drain(stage)
-    for copy in halos + pre_halos:
-        copy.wait_send()
-    for store in stores:
-        store.wait()
-
-
-def deliver(*refs):
-    sources, targets, held, (in_sem, out_sem) = refs[:4], refs[4:8], refs[8:12], refs[12:]
-    loads = [pltpu.make_async_copy(sources[i], held[i], in_sem.at[i]) for i in range(4)]
-    stores = [pltpu.make_async_copy(held[i], targets[i], out_sem.at[i]) for i in range(4)]
-    for load in loads:
-        load.start()
-    for load, store in zip(loads, stores):
-        load.wait()
-        store.start()
+    for i in (0, 1):
+        loads[i].wait()
+        stores[i].start()
     for store in stores:
         store.wait()
 
@@ -429,8 +438,8 @@
         out_shape=(
             jax.ShapeDtypeStruct((C, 2, PLANE), BF16),
             jax.ShapeDtypeStruct((C, 2, PLANE), BF16),
-            jax.ShapeDtypeStruct((2 * KZ, C, C), F32),
-            jax.ShapeDtypeStruct((27 * C, C), F32),
+            jax.ShapeDtypeStruct((KZ, C, 128), F32),
+            jax.ShapeDtypeStruct((32, 32, 128), BF16),
         ),
         in_specs=[any_space] * 8,
         out_specs=(any_space,) * 4,
@@ -445,8 +454,7 @@
             vmem((16, PLANE), BF16),
             vmem((C, 2, PLANE), BF16),
             vmem((C, 2, PLANE), BF16),
-            vmem((2 * KZ, C, C), F32),
-            vmem((27 * C, C), F32),
+            vmem((KZ, C, 128), F32),
             vmem((8, G, 16, 128), BF16),
             vmem((8, G, 16, 128), BF16),
             vmem((2, C, PLANE), BF16),
@@ -493,10 +501,16 @@
     outs = pl.pallas_call(
         deliver,
         name="deliver",
-        out_shape=tuple(jax.ShapeDtypeStruct(out.shape, out.dtype) for out in outs),
+        out_shape=(
+            jax.ShapeDtypeStruct((C, 2, PLANE), BF16),
+            jax.ShapeDtypeStruct((C, 2, PLANE), BF16),
+            jax.ShapeDtypeStruct((2 * KZ, C, C), F32),
+            jax.ShapeDtypeStruct((27 * C, C), F32),
+        ),
         in_specs=[any_space] * 4,
         out_specs=(any_space,) * 4,
-        scratch_shapes=[vmem(out.shape, out.dtype) for out in outs] + [dma((4,)), dma((4,))],
+        scratch_shapes=[vmem(out.shape, out.dtype) for out in outs]
+        + [vmem((2 * KZ, C, C), F32), vmem((27 * C, C), F32), dma((4,)), dma((4,))],
         compiler_params=pltpu.CompilerParams(vmem_limit_bytes=60 << 20),
     )(*outs)
     activated, input_gradient, mode_gradient, conv_gradient = outs

time: 61.4 us -> 60.5 us (0.985)
  Pallas kernels: 60.5 us -> 59.8 us
    pallas_call x1, Pallas kernels: 57.9 us -> 57.2 us  [shards(): pl.pallas_call(kernel, name='layer', out_shape=(jax.ShapeDtypeStruct((C,...]
where the time goes in v4:
time: 60.5 us; the launch traced here: 60.4 us
  Pallas kernels  59.8 us (99%)
  between operations  0.64 us (1%)
    pallas_call x1, Pallas kernels, shards(): pl.pallas_call(kernel, name='layer', out_shape=(jax.ShapeDtypeStruct((C,...  57.2 us
    pallas_call x1, Pallas kernels, shards(): pl.pallas_call(deliver, name='deliver', out_shape=(jax.ShapeDtypeStruct((...  2.57 us

profile of v4, /device:TPU:1, one launch (start us, length us, event | category | flops | bytes accessed | tf_op | source)
XLA Modules:
  0.0 60.4 jit_solution(11167052518842108979)
XLA Ops:
  0.6 57.2 %layer.1 = (bf16[64,2,1024]{2,1,0:T(2,128)(2,1)}, bf16[64,2,1024]{2,1,0:T(2,128)(2,1)}, f32[12,64,128]{2,1,0:T(8,128)}, bf16[32,32,128]{2,1,0:T(8,128)(2,1)}) custom-call(bf16[64,2,1024]{2,1,0:T(2,128)(2,1)} %bitcast.10, bf16[64,2,1024]{2,1,0:T(2,128)(2,1)} %bitcast.11, bf16[24,64,64]{2,1,0:T(8,128)(2,1)} %bitcast.9, bf16[3,9,64,64]{3,2,1,0:T(8,128)(2,1)} %bitcast.8, ...), custom_call_target="tpu_custom_call" | custom-call | tf_op jit(solution)/shard_map/layer/pallas_call | solution.py:435
  57.8 2.6 %deliver.1 = (bf16[64,2,1024]{2,1,0:T(2,128)(2,1)}, bf16[64,2,1024]{2,1,0:T(2,128)(2,1)}, f32[24,64,64]{2,1,0:T(8,128)}, f32[1728,64]{1,0:T(8,128)}) custom-call(bf16[64,2,1024]{2,1,0:T(2,128)(2,1)} %get-tuple-element.12.act_in, bf16[64,2,1024]{2,1,0:T(2,128)(2,1)} %get-tuple-element.13.grad_in, f32[12,64,128]{2,1,0:T(8,128)} %get-tuple-element.14.mode_in, ...), custom_call_target="tpu_custom_call" | custom-call | tf_op jit(solution)/shard_map/deliver/pallas_call | solution.py:501

commit v5 on v4

--- a/solution.py
+++ b/solution.py
@@ -108,8 +108,17 @@
     for load in loads:
         load.start()
 
-    def peer_of(axis, i):
-        return lax.rem(mine[axis] + 1 + i, G)
+    def peers_of(axis):
+        if axis == "space":
+            order = [(z, y) for z in (4, 3, 5, 2, 6, 1, 7, 0) for y in (1, 0)][:-1]
+            return [lax.rem(me_s // 2 + z, 8) * 2 + lax.rem(me_s + y, 2) for z, y in order]
+        order = [(x, y, c) for y in (1, 0) for x in (2, 1, 3, 0) for c in (1, 0)][:-1]
+        return [
+            lax.rem(me_b // 4 + x, 4) * 4 + lax.rem(me_b // 2 + y, 2) * 2 + lax.rem(me_b + c, 2)
+            for x, y, c in order
+        ]
+
+    partners = {axis: peers_of(axis) for axis in ("space", "batch")}
 
     def tile_copy(phase, axis, source, slot):
         return pltpu.make_async_remote_copy(
@@ -125,11 +134,8 @@
         me = mine[axis]
         send[phase] = value.reshape(G, 16, 128)
 
-        def step(i, carry):
-            tile_copy(phase, axis, peer_of(axis, i), me).start()
-            return carry
-
-        lax.fori_loop(0, G - 1, step, 0)
+        for peer in partners[axis]:
+            tile_copy(phase, axis, peer, me).start()
         recv[phase, me] = send[phase, me]
 
     def all_bytes(buffer, sem):

time: 60.5 us -> 59.4 us (0.982)
  Pallas kernels: 59.8 us -> 58.6 us
    pallas_call x1, Pallas kernels: 57.2 us -> 56.1 us  [shards(): pl.pallas_call(kernel, name='layer', out_shape=(jax.ShapeDtypeStruct((C,...]
where the time goes in v5:
time: 59.4 us; the launch traced here: 59.3 us
  Pallas kernels  58.6 us (99%)
  between operations  0.64 us (1%)
    pallas_call x1, Pallas kernels, shards(): pl.pallas_call(kernel, name='layer', out_shape=(jax.ShapeDtypeStruct((C,...  56.1 us
    pallas_call x1, Pallas kernels, shards(): pl.pallas_call(deliver, name='deliver', out_shape=(jax.ShapeDtypeStruct((...  2.57 us

profile of v5, /device:TPU:1, one launch (start us, length us, event | category | flops | bytes accessed | tf_op | source)
XLA Modules:
  0.0 59.3 jit_solution(17255596148176275170)
XLA Ops:
  0.6 56.1 %layer.1 = (bf16[64,2,1024]{2,1,0:T(2,128)(2,1)}, bf16[64,2,1024]{2,1,0:T(2,128)(2,1)}, f32[12,64,128]{2,1,0:T(8,128)}, bf16[32,32,128]{2,1,0:T(8,128)(2,1)}) custom-call(bf16[64,2,1024]{2,1,0:T(2,128)(2,1)} %bitcast.10, bf16[64,2,1024]{2,1,0:T(2,128)(2,1)} %bitcast.11, bf16[24,64,64]{2,1,0:T(8,128)(2,1)} %bitcast.9, bf16[3,9,64,64]{3,2,1,0:T(8,128)(2,1)} %bitcast.8, ...), custom_call_target="tpu_custom_call" | custom-call | tf_op jit(solution)/shard_map/layer/pallas_call | solution.py:441
  56.7 2.6 %deliver.1 = (bf16[64,2,1024]{2,1,0:T(2,128)(2,1)}, bf16[64,2,1024]{2,1,0:T(2,128)(2,1)}, f32[24,64,64]{2,1,0:T(8,128)}, f32[1728,64]{1,0:T(8,128)}) custom-call(bf16[64,2,1024]{2,1,0:T(2,128)(2,1)} %get-tuple-element.12.act_in, bf16[64,2,1024]{2,1,0:T(2,128)(2,1)} %get-tuple-element.13.grad_in, f32[12,64,128]{2,1,0:T(8,128)} %get-tuple-element.14.mode_in, ...), custom_call_target="tpu_custom_call" | custom-call | tf_op jit(solution)/shard_map/deliver/pallas_call | solution.py:507

commit v6 on v5

--- a/solution.py
+++ b/solution.py
@@ -308,7 +308,7 @@
         count, me, device, source, target = stages[stage]
         target[me] = source(me)[...]
 
-        def step(i, carry):
+        for i in sorted(range(1, count), key=lambda i: -min(i, count - i)):
             peer = lax.rem(me + i, count)
             pltpu.make_async_remote_copy(
                 src_ref=source(peer),
@@ -318,9 +318,6 @@
                 device_id=device(peer),
                 device_id_type=MESH,
             ).start()
-            return carry
-
-        lax.fori_loop(1, count, step, 0)
 
     def sum_wait(stage):
         all_bytes(stages[stage][4], sum_recv_sem.at[stage])

time: 59.4 us -> 59 us (level)
  Pallas kernels: 58.6 us -> 57.9 us
    pallas_call x1, Pallas kernels: 56.1 us -> 55.4 us  [shards(): pl.pallas_call(kernel, name='layer', out_shape=(jax.ShapeDtypeStruct((C,...]
where the time goes in v6:
time: 59 us; the launch traced here: 58.6 us
  Pallas kernels  57.9 us (98%)
  between operations  0.64 us (1%)
    pallas_call x1, Pallas kernels, shards(): pl.pallas_call(kernel, name='layer', out_shape=(jax.ShapeDtypeStruct((C,...  55.4 us
    pallas_call x1, Pallas kernels, shards(): pl.pallas_call(deliver, name='deliver', out_shape=(jax.ShapeDtypeStruct((...  2.57 us

profile of v6, /device:TPU:1, one launch (start us, length us, event | category | flops | bytes accessed | tf_op | source)
XLA Modules:
  0.0 58.6 jit_solution(9119952774411447109)
XLA Ops:
  0.6 55.4 %layer.1 = (bf16[64,2,1024]{2,1,0:T(2,128)(2,1)}, bf16[64,2,1024]{2,1,0:T(2,128)(2,1)}, f32[12,64,128]{2,1,0:T(8,128)}, bf16[32,32,128]{2,1,0:T(8,128)(2,1)}) custom-call(bf16[64,2,1024]{2,1,0:T(2,128)(2,1)} %bitcast.10, bf16[64,2,1024]{2,1,0:T(2,128)(2,1)} %bitcast.11, bf16[24,64,64]{2,1,0:T(8,128)(2,1)} %bitcast.9, bf16[3,9,64,64]{3,2,1,0:T(8,128)(2,1)} %bitcast.8, ...), custom_call_target="tpu_custom_call" | custom-call | tf_op jit(solution)/shard_map/layer/pallas_call | solution.py:438
  56.0 2.6 %deliver.1 = (bf16[64,2,1024]{2,1,0:T(2,128)(2,1)}, bf16[64,2,1024]{2,1,0:T(2,128)(2,1)}, f32[24,64,64]{2,1,0:T(8,128)}, f32[1728,64]{1,0:T(8,128)}) custom-call(bf16[64,2,1024]{2,1,0:T(2,128)(2,1)} %get-tuple-element.12.act_in, bf16[64,2,1024]{2,1,0:T(2,128)(2,1)} %get-tuple-element.13.grad_in, f32[12,64,128]{2,1,0:T(8,128)} %get-tuple-element.14.mode_in, ...), custom_call_target="tpu_custom_call" | custom-call | tf_op jit(solution)/shard_map/deliver/pallas_call | solution.py:504
